TPU v7x, 128 devices: a whole 4x4x4 slice. The times are simulated.
128 devices in a mesh: front: 4 (over y), prow: 4 (over x), pcol: 8 (over z, core).
Axes of the slice: x: 4, y: 4, z: 4, core: 2. Of those that a mesh axis runs over, the one named last changes fastest.
Arguments:
- base_front: float32 [4, 8192, 8192], P('front', 'prow', 'pcol'), as said below
- child_tiles: float32 [16384, 4096], P(('front', 'prow', 'pcol')), may hold values from -4 to 4
- tile_target: int32 [16384, 3], P(('front', 'prow', 'pcol')), may hold values from 0 to 127, as said below
- fill_pattern: int32 [4, 128, 128], P('front', 'prow', 'pcol'), may hold values from 0 to 1, as said below
Outputs:
- front_out: float32 [4, 8192, 8192], P('front', 'prow', 'pcol')
- panel_factor: float32 [4, 8192, 256], P('front', 'prow')
Inputs may be any that keep to these rules, and one draw needn't show every extreme that they name: tile_target[t, 0] is a front and tile_target[t, 1], tile_target[t, 2] are block indices below 128. The child blocks of one device go to at most 2 per device of the parent grids (the device of front f holding block row i and block column j is the one at prow i // (128 // 4), pcol j // (128 // 8)); every device sends exactly 2 to some device. No child block lands where both block indices are below 4. `fill_pattern`: whole block rows and columns of a front may be empty. `base_front`: the symmetric part of each front's leading 256 x 256 block is positive definite.
All inputs are finite; a program needn't handle non-finite values.
Results may differ from a plain program's by a relative error of at most 0.0003.
Values sent between devices are 32-bit elements; how exact they have to be, the bound alone decides.
A program may use at most 128 MiB of HBM per device.

v0:
```python
import jax
import jax.numpy as jnp
from jax import lax
from jax.experimental import pallas as pl
from jax.experimental.pallas import tpu as pltpu
from jax.sharding import PartitionSpec as P

BLK = 64
PW = 256
DEV = 128
HELD = 128
ROWS = 2048
COLS = 1024
SLOT = 72
SENT = 65
CHUNK = 128
NCH = 8
LAG = 2
MESH = pl.DeviceIdType.MESH
F32 = jnp.float32
BF16 = jnp.bfloat16
HI = lax.Precision.HIGHEST


def split2(x):
    hi = x.astype(BF16)
    return hi, (x - hi.astype(F32)).astype(BF16)


def dot_nt(a, b):
    return lax.dot_general(a, b, (((1,), (1,)), ((), ())), preferred_element_type=F32)


def dot_nn(a, b):
    return lax.dot_general(a, b, (((1,), (0,)), ((), ())), preferred_element_type=F32)


def relayout_tiles(child_ref, tall):
    low = lax.broadcasted_iota(jnp.int32, (8, 128), 1) < BLK

    def group(g, carry):
        base = pl.multiple_of(g * 8, 8)
        for k in range(32):
            v = child_ref[pl.ds(base, 8), k * 128 : (k + 1) * 128]
            w = pltpu.roll(v, 64, 1)
            tall[pl.ds(g * 512 + 2 * k, 8, stride=64), :] = jnp.where(low, v, w)
            tall[pl.ds(g * 512 + 2 * k + 1, 8, stride=64), :] = jnp.where(low, w, v)
        return carry

    lax.fori_loop(0, HELD // 8, group, 0)


def half_inverse(a, aw, ew):
    aw[...] = a
    row = lax.broadcasted_iota(jnp.int32, (128, 128), 0)
    col = lax.broadcasted_iota(jnp.int32, (128, 128), 1)
    ew[...] = (row == col).astype(F32)
    sub = lax.broadcasted_iota(jnp.int32, (8, 128), 0)

    def step(g, carry):
        top = pl.multiple_of(g * 8, 8)
        xa = aw[pl.ds(top, 8), :]
        xe = ew[pl.ds(top, 8), :]
        c = [jnp.broadcast_to(xa[:, m : m + 1], (8, 128)) for m in range(8)]
        scale = []
        lower = {}
        ra = []
        re = []
        for k in range(8):
            rs = lax.rsqrt(jnp.broadcast_to(c[k][k : k + 1, :], (8, 128)))
            p = jnp.broadcast_to(c[k][k : k + 1, :], (8, 128))
            rs = rs * (1.5 - 0.5 * p * rs * rs)
            scale.append(rs)
            lk = c[k] * rs
            below = jnp.where(sub > k, lk, 0.0)
            for m in range(k + 1, 8):
                lmk = jnp.broadcast_to(lk[m : m + 1, :], (8, 128))
                lower[m, k] = lmk
                c[m] = c[m] - below * lmk
            row_a = jnp.broadcast_to(xa[k : k + 1, :], (8, 128)) * rs
            row_e = jnp.broadcast_to(xe[k : k + 1, :], (8, 128)) * rs
            ra.append(row_a)
            re.append(row_e)
            xa = xa - below * row_a
            xe = jnp.where(sub == k, row_e, xe - below * row_e)
        ew[pl.ds(top, 8), :] = xe
        for q in range(16):
            ya = aw[q * 8 : q * 8 + 8, :]
            ye = ew[q * 8 : q * 8 + 8, :]
            live = jnp.where(q > g, 1.0, 0.0).astype(F32)
            d = [jnp.broadcast_to(ya[:, m : m + 1], (8, 128)) * live for m in range(8)]
            for k in range(8):
                lk = d[k] * scale[k]
                for m in range(k + 1, 8):
                    d[m] = d[m] - lk * lower[m, k]
                ya = ya - lk * ra[k]
                ye = ye - lk * re[k]
            aw[q * 8 : q * 8 + 8, :] = pltpu.roll(ya, 120, 1)
            ew[q * 8 : q * 8 + 8, :] = ye
        return carry

    lax.fori_loop(0, 16, step, 0)


def pivot_inverse(lead, inv_t, aw, ew):
    a11 = lead[0:128, 0:128]
    a21 = 0.5 * (lead[128:256, 0:128] + lead[0:128, 128:256].T)
    a22 = lead[128:256, 128:256]
    half_inverse(0.5 * (a11 + a11.T), aw, ew)
    e1 = ew[...]
    l21 = lax.dot_general(a21, e1, (((1,), (1,)), ((), ())), precision=HI, preferred_element_type=F32)
    s = 0.5 * (a22 + a22.T) - lax.dot_general(
        l21, l21, (((1,), (1,)), ((), ())), precision=HI, preferred_element_type=F32
    )
    inv_t[0:128, 0:128] = e1.T
    w = jnp.dot(l21, e1, precision=HI, preferred_element_type=F32)
    half_inverse(s, aw, ew)
    e2 = ew[...]
    inv_t[0:128, 128:256] = -jnp.dot(e2, w, precision=HI, preferred_element_type=F32).T
    inv_t[128:256, 128:256] = e2.T
    inv_t[128:256, 0:128] = jnp.zeros((128, 128), F32)


def assemble_panel(recv_v, panels):
    lane = lax.broadcasted_iota(jnp.int32, (128, 128), 1)
    low = lane < BLK
    low32 = lax.broadcasted_iota(jnp.int32, (32, 128), 1) < BLK
    place = recv_v[pl.ds(BLK, DEV, stride=SLOT), :].T
    row = lax.broadcasted_iota(jnp.int32, (128, 128), 0)
    want = (lax.rem(row, 32) * 16 + row // 32).astype(F32)
    hot = jnp.concatenate(
        [
            (want == jnp.broadcast_to(place[0:1, :], (128, 128))).astype(BF16),
            (want == jnp.broadcast_to(place[BLK : BLK + 1, :], (128, 128))).astype(BF16),
        ],
        axis=1,
    )

    def quad(i, carry):
        sides = []
        for u in range(2):
            x0 = recv_v[pl.ds(4 * i + 2 * u, DEV, stride=SLOT), :]
            x1 = recv_v[pl.ds(4 * i + 2 * u + 1, DEV, stride=SLOT), :]
            first = jnp.where(low, x0, pltpu.roll(x1, 64, 1))
            second = jnp.where(low, pltpu.roll(x0, 64, 1), x1)
            sides.append(jnp.concatenate([first, second], axis=0))
        x = jnp.concatenate(sides, axis=1)
        hi, lo = split2(x)
        lo2 = (x - hi.astype(F32) - lo.astype(F32)).astype(BF16)
        y = dot_nn(hot, hi) + dot_nn(hot, lo) + dot_nn(hot, lo2)
        for u in range(2):
            part = y[:, u * 128 : (u + 1) * 128]
            for b in range(2):
                even = part[b * 64 : b * 64 + 32, :]
                odd = part[b * 64 + 32 : b * 64 + 64, :]
                add0 = jnp.where(low32, even, pltpu.roll(odd, 64, 1))
                add1 = jnp.where(low32, pltpu.roll(even, 64, 1), odd)
                for v, add in ((0, add0), (1, add1)):
                    rows = pl.ds(4 * i + 2 * u + v, 32, stride=BLK)
                    panels[b][rows, :] = panels[b][rows, :] + add
        return carry

    lax.fori_loop(0, 16, quad, 0)


def exchange_kernel(
    idx_ref,
    meta_ref,
    child_ref,
    base_ref,
    recv_ref,
    l_ref,
    lc_ref,
    tall,
    out,
    recv_v,
    panel0,
    panel1,
    lead,
    inv_t,
    aw,
    ew,
    lchunk,
    tile_send,
    tile_recv,
    lead_send,
    lead_recv,
    own_recv,
    oth_recv,
    x_recv,
    z_send,
    c_send,
    x_send,
    local,
):
    f = lax.axis_index("front")
    r = lax.axis_index("prow")
    c = lax.axis_index("pcol")
    z = c // 2
    h = lax.rem(c, 2)
    me = (f * 4 + r) * 8 + c

    def where_is(d):
        return (d // 32, lax.rem(d // 8, 4), lax.rem(d, 8))

    barrier = pltpu.get_barrier_semaphore()

    def greet(k, carry):
        pl.semaphore_signal(
            barrier, inc=1, device_id=where_is(lax.rem(me + k, DEV)), device_id_type=MESH
        )
        return carry

    lax.fori_loop(1, DEV, greet, 0)

    lead_in = pltpu.make_async_copy(base_ref.at[0, pl.ds(0, PW), pl.ds(0, PW)], lead, local.at[0])
    panel_in0 = pltpu.make_async_copy(base_ref.at[0, :, pl.ds(0, 128)], panel0, local.at[1])
    panel_in1 = pltpu.make_async_copy(base_ref.at[0, :, pl.ds(128, 128)], panel1, local.at[2])
    first_col = c == 0

    @pl.when(first_col)
    def _():
        panel_in0.start()
        panel_in1.start()

        @pl.when(r == 0)
        def _():
            lead_in.start()

    relayout_tiles(child_ref, tall.reshape(HELD * BLK, 128))
    pl.semaphore_wait(barrier, DEV - 1)

    def lead_copy(j):
        return pltpu.make_async_remote_copy(
            src_ref=lead,
            dst_ref=lead,
            send_sem=lead_send.at[j - 1],
            recv_sem=lead_recv,
            device_id=(f, j, 0),
            device_id_type=MESH,
        )

    @pl.when(first_col & (r == 0))
    def _():
        lead_in.wait()
        for j in range(1, 4):
            lead_copy(j).start()

    low = lax.broadcasted_iota(jnp.int32, (BLK, 128), 1) < BLK

    def fill_slot(d):
        out[d, 0:BLK, :] = jnp.where(low, tall[idx_ref[2 * d]], tall[idx_ref[2 * d + 1]])
        out[d, pl.ds(BLK, 1), :] = meta_ref[pl.ds(d, 1), :]

    def send(tf, tr, tc):
        d = (tf * 4 + tr) * 8 + tc
        fill_slot(d)
        pltpu.make_async_remote_copy(
            src_ref=out.at[d, pl.ds(0, SENT)],
            dst_ref=recv_ref.at[me, pl.ds(0, SENT)],
            send_sem=tile_send,
            recv_sem=tile_recv,
            device_id=(tf, tr, tc),
            device_id_type=MESH,
        ).start()

    def send_first(k):
        a = lax.rem(k, 4)
        b = lax.rem(a + k // 4, 4)
        tf, tr = lax.rem(f + a, 4), lax.rem(r + b, 4)

        @pl.when((tf != f) | (tr != r) | (c != 0))
        def _():
            send(tf, tr, 0)

    def send_rest(k):
        a = lax.rem(k, 4)
        jk = lax.rem(k // 4, 16)
        b = lax.rem(a + lax.rem(jk, 4), 4)
        dz = lax.rem(a + jk // 4, 4)
        tf, tr = lax.rem(f + a, 4), lax.rem(r + b, 4)
        tc = lax.rem(z + dz, 4) * 2 + lax.rem(h + k // 64, 2)

        @pl.when((tc != 0) & ((tf != f) | (tr != r) | (tc != c)))
        def _():
            send(tf, tr, tc)

    def phase_one(k, carry):
        send_first(k)
        send_rest(k)
        return carry

    def phase_two(k, carry):
        send_rest(k)
        return carry

    lax.fori_loop(0, 16, phase_one, 0)
    lax.fori_loop(16, DEV, phase_two, 0)
    fill_slot(me)
    own_tiles = pltpu.make_async_copy(
        out.at[me, pl.ds(0, SENT)], recv_ref.at[me, pl.ds(0, SENT)], local.at[3]
    )
    own_tiles.start()
    own_tiles.wait()

    all_tiles = pltpu.make_async_copy(
        recv_ref.at[pl.ds(0, DEV - 1), pl.ds(0, SENT)],
        recv_ref.at[pl.ds(0, DEV - 1), pl.ds(0, SENT)],
        tile_recv,
    )

    def piece(half, k):
        return pl.ds(pl.multiple_of(half * COLS + k * CHUNK, CHUNK), CHUNK)

    def strip(k):
        return pl.ds(pl.multiple_of(k * CHUNK, CHUNK), CHUNK)

    def push(rows, send_sem, recv_sem, target):
        return pltpu.make_async_remote_copy(
            src_ref=l_ref.at[rows],
            dst_ref=l_ref.at[rows],
            send_sem=send_sem,
            recv_sem=recv_sem,
            device_id=target,
            device_id_type=MESH,
        )

    def z_next(half, k):
        nz = lax.rem(z + 1 + 2 * half, 4)
        return push(
            piece(half, k), z_send.at[half * NCH + k], own_recv.at[k], (f, r, nz * 2 + half)
        )

    def cross(half, k, recv_sem):
        return push(piece(half, k), c_send.at[half * NCH + k], recv_sem, (f, r, z * 2 + 1 - h))

    def x_hop(src, k):
        nr = lax.rem(r + 1 + 2 * lax.rem(k, 2), 4)
        return pltpu.make_async_remote_copy(
            src_ref=src,
            dst_ref=lc_ref.at[strip(k)],
            send_sem=x_send.at[k],
            recv_sem=x_recv.at[k],
            device_id=(f, nr, c),
            device_id_type=MESH,
        )

    x_root = r == z
    x_dist = lax.rem(r - z + 4, 4)

    def lc_local(k):
        return pltpu.make_async_copy(l_ref.at[piece(h, k)], lc_ref.at[strip(k)], local.at[4])

    def x_forwards(k):
        return jnp.where(lax.rem(k, 2) == 0, x_dist != 3, x_dist != 1)

    def x_start(k):
        x_hop(l_ref.at[piece(h, k)], k).start()
        own = lc_local(k)
        own.start()
        own.wait()

    def x_pass(k):
        x_hop(lc_ref.at[strip(k)], k).wait_recv()

        @pl.when(x_forwards(k))
        def _():
            x_hop(lc_ref.at[strip(k)], k).start()

    @pl.when(first_col)
    def _():
        @pl.when(r != 0)
        def _():
            lead_copy(1).wait_recv()

        pivot_inverse(lead, inv_t, aw, ew)
        all_tiles.wait()
        panel_in0.wait()
        panel_in1.wait()

        def fetch(i, carry):
            pltpu.make_async_copy(
                recv_ref.at[i, pl.ds(0, SENT)],
                recv_v.at[pl.ds(pl.multiple_of(i * SLOT, 8), SENT)],
                local.at[5],
            ).start()
            return carry

        lax.fori_loop(0, DEV, fetch, 0)

        pltpu.make_async_copy(
            recv_ref.at[:, pl.ds(0, SENT)], recv_ref.at[:, pl.ds(0, SENT)], local.at[5]
        ).wait()
        assemble_panel(recv_v, (panel0, panel1))

        def produce(k, carry):
            for half in range(2):
                rows = piece(half, k)
                p = jnp.concatenate([panel0[rows, :], panel1[rows, :]], axis=1)
                lchunk[half] = jnp.dot(p, inv_t[...], precision=HI, preferred_element_type=F32)
                keep = pltpu.make_async_copy(lchunk.at[half], l_ref.at[rows], local.at[6])
                keep.start()
                keep.wait()
                z_next(half, k).start()
            cross(0, k, oth_recv.at[k]).start()
            cross(1, k, own_recv.at[k]).start()

            @pl.when(x_root)
            def _():
                x_start(k)

            return carry

        lax.fori_loop(0, NCH, produce, 0)

        @pl.when(r != 0)
        def _():
            def take(k, carry):
                x_pass(k)
                return carry

            lax.fori_loop(0, NCH, take, 0)

    z_forwards = ((h == 0) & ((z == 1) | (z == 2))) | ((h == 1) & ((z == 3) | (z == 2)))

    @pl.when(jnp.logical_not(first_col))
    def _():
        def relay(k, carry):
            @pl.when(k < NCH)
            def _():
                z_next(h, k).wait_recv()

                @pl.when(z_forwards)
                def _():
                    z_next(h, k).start()

                @pl.when(z != 0)
                def _():
                    cross(h, k, oth_recv.at[k]).start()

                @pl.when(x_root)
                def _():
                    x_start(k)

            @pl.when((k >= LAG) & jnp.logical_not(x_root))
            def _():
                x_pass(k - LAG)

            return carry

        lax.fori_loop(0, NCH + LAG, relay, 0)

        def other(k, carry):
            cross(1 - h, k, oth_recv.at[k]).wait_recv()
            return carry

        lax.fori_loop(0, NCH, other, 0)
        all_tiles.wait()

    pltpu.make_async_copy(
        out.at[pl.ds(0, DEV - 1), pl.ds(0, SENT)],
        out.at[pl.ds(0, DEV - 1), pl.ds(0, SENT)],
        tile_send,
    ).wait()

    @pl.when(first_col & (r == 0))
    def _():
        for j in range(1, 4):
            lead_copy(j).wait_send()

    def drain(k, carry):
        @pl.when(first_col)
        def _():
            for half in range(2):
                z_next(half, k).wait_send()
                cross(half, k, own_recv.at[k]).wait_send()

        @pl.when(z_forwards)
        def _():
            z_next(h, k).wait_send()

        @pl.when(z != 0)
        def _():
            cross(h, k, own_recv.at[k]).wait_send()

        @pl.when(x_root | x_forwards(k))
        def _():
            x_hop(lc_ref.at[strip(k)], k).wait_send()

        return carry

    lax.fori_loop(0, NCH, drain, 0)


def exchange(idx, meta, child_tiles, base_front):
    return pl.pallas_call(
        exchange_kernel,
        out_shape=(
            jax.ShapeDtypeStruct((DEV, SLOT, 128), F32),
            jax.ShapeDtypeStruct((ROWS, PW), F32),
            jax.ShapeDtypeStruct((COLS, PW), F32),
        ),
        in_specs=[
            pl.BlockSpec(memory_space=pltpu.SMEM),
            pl.BlockSpec(memory_space=pltpu.VMEM),
            pl.BlockSpec(memory_space=pltpu.VMEM),
            pl.BlockSpec(memory_space=pl.ANY),
        ],
        out_specs=(
            pl.BlockSpec(memory_space=pl.ANY),
            pl.BlockSpec(memory_space=pl.ANY),
            pl.BlockSpec(memory_space=pl.ANY),
        ),
        scratch_shapes=[
            pltpu.VMEM((HELD, BLK, 128), F32),
            pltpu.VMEM((DEV, SLOT, 128), F32),
            pltpu.VMEM((DEV * SLOT, 128), F32),
            pltpu.VMEM((ROWS, 128), F32),
            pltpu.VMEM((ROWS, 128), F32),
            pltpu.VMEM((PW, PW), F32),
            pltpu.VMEM((PW, PW), F32),
            pltpu.VMEM((128, 128), F32),
            pltpu.VMEM((128, 128), F32),
            pltpu.VMEM((2, CHUNK, PW), F32),
            pltpu.SemaphoreType.DMA(()),
            pltpu.SemaphoreType.DMA(()),
            pltpu.SemaphoreType.DMA((3,)),
            pltpu.SemaphoreType.DMA(()),
            pltpu.SemaphoreType.DMA((NCH,)),
            pltpu.SemaphoreType.DMA((NCH,)),
            pltpu.SemaphoreType.DMA((NCH,)),
            pltpu.SemaphoreType.DMA((2 * NCH,)),
            pltpu.SemaphoreType.DMA((2 * NCH,)),
            pltpu.SemaphoreType.DMA((NCH,)),
            pltpu.SemaphoreType.DMA((8,)),
        ],
        compiler_params=pltpu.CompilerParams(
            collective_id=0, has_side_effects=True, vmem_limit_bytes=48 << 20
        ),
    )(idx, meta, child_tiles, base_front)


STEP = 256


def update_kernel(
    base_ref, recv_ref, l_ref, lc_ref, fill_ref, front_ref, factor_ref, acc, tiles, lv, lcv, lc_hi, lc_lo, keep, place, base_in, out_sem, sems
):
    r = lax.axis_index("prow")
    c = lax.axis_index("pcol")
    steps = ROWS // STEP

    def strip(i):
        return pl.ds(pl.multiple_of(i * STEP, STEP), STEP)

    def load(i):
        return pltpu.make_async_copy(base_ref.at[0, strip(i)], acc.at[strip(i)], base_in.at[i])

    def store(i):
        return pltpu.make_async_copy(acc.at[strip(i)], front_ref.at[0, strip(i)], out_sem.at[i])

    l_in = pltpu.make_async_copy(l_ref, lv, sems.at[0])
    lc_in = pltpu.make_async_copy(lc_ref, lcv, sems.at[1])
    tiles_in = pltpu.make_async_copy(
        recv_ref.at[:, pl.ds(0, BLK)], tiles, sems.at[2]
    )
    place_in = pltpu.make_async_copy(recv_ref.at[:, BLK], place, sems.at[3])
    lc_in.start()
    l_in.start()
    for i in range(steps):
        load(i).start()
    place_in.start()
    tiles_in.start()
    row_block = lax.broadcasted_iota(jnp.int32, (32, 16), 0) + 32 * r
    col_block = lax.broadcasted_iota(jnp.int32, (32, 16), 1) + 16 * c
    on = (fill_ref[0] > 0) & (row_block >= PW // BLK) & (col_block >= PW // BLK)
    spread = (
        lax.broadcasted_iota(jnp.int32, (16, COLS), 1) // BLK
        == lax.broadcasted_iota(jnp.int32, (16, COLS), 0)
    ).astype(BF16)
    keep[...] = dot_nn(on.astype(BF16), spread)
    lc_in.wait()
    hi, lo = split2(lcv[...])
    lc_hi[...] = hi
    lc_lo[...] = lo
    l_in.wait()
    factor_out = pltpu.make_async_copy(lv, factor_ref.at[0], sems.at[4])
    factor_out.start()

    def product(i, carry):
        load(i).wait()
        a_hi, a_lo = split2(lv[strip(i), :])
        p = dot_nt(a_hi, lc_hi[...]) + dot_nt(a_hi, lc_lo[...]) + dot_nt(a_lo, lc_hi[...])
        for b in range(STEP // BLK):
            rows = pl.ds(pl.multiple_of(i * STEP + b * BLK, BLK), BLK)
            mask = jnp.broadcast_to(keep[pl.ds(i * (STEP // BLK) + b, 1), :], (BLK, COLS))
            acc[rows, :] = acc[rows, :] - p[b * BLK : (b + 1) * BLK, :] * mask
        return carry

    lax.fori_loop(0, steps, product, 0)
    place_in.wait()
    tiles_in.wait()
    half = lax.broadcasted_iota(jnp.int32, (BLK, 128), 1) // BLK

    def add(s, carry):
        for u in range(2):
            p = place[s, u * BLK].astype(jnp.int32)

            @pl.when(p >= 0)
            def _():
                rb = lax.shift_right_logical(p, 4)
                cb = jnp.bitwise_and(p, 15)
                side = jnp.bitwise_and(cb, 1)
                t = tiles[s]
                moved = pltpu.roll(t, 64, 1)
                v = jnp.where(side == u, t, moved)
                v = jnp.where(half == side, v, 0.0)
                rows = pl.ds(pl.multiple_of(rb * BLK, BLK), BLK)
                cols = pl.ds(pl.multiple_of(lax.shift_right_logical(cb, 1) * 128, 128), 128)
                acc[rows, cols] = acc[rows, cols] + v

        return carry

    lax.fori_loop(0, DEV, add, 0)
    for i in range(steps):
        store(i).start()
    factor_out.wait()
    for i in range(steps):
        store(i).wait()


def update(base_front, recv, l, lc, fill_pattern):
    return pl.pallas_call(
        update_kernel,
        out_shape=(
            jax.ShapeDtypeStruct((1, ROWS, COLS), F32),
            jax.ShapeDtypeStruct((1, ROWS, PW), F32),
        ),
        in_specs=[pl.BlockSpec(memory_space=pl.ANY)] * 4
        + [pl.BlockSpec(memory_space=pltpu.VMEM)],
        out_specs=(pl.BlockSpec(memory_space=pl.ANY), pl.BlockSpec(memory_space=pl.ANY)),
        scratch_shapes=[
            pltpu.VMEM((ROWS, COLS), F32),
            pltpu.VMEM((DEV, BLK, 128), F32),
            pltpu.VMEM((ROWS, PW), F32),
            pltpu.VMEM((COLS, PW), F32),
            pltpu.VMEM((COLS, PW), BF16),
            pltpu.VMEM((COLS, PW), BF16),
            pltpu.VMEM((32, COLS), F32),
            pltpu.SMEM((DEV, 128), F32),
            pltpu.SemaphoreType.DMA((ROWS // STEP,)),
            pltpu.SemaphoreType.DMA((ROWS // STEP,)),
            pltpu.SemaphoreType.DMA((5,)),
        ],
        compiler_params=pltpu.CompilerParams(vmem_limit_bytes=40 << 20),
    )(base_front, recv, l, lc, fill_pattern)


def slots(tile_target):
    block_row = tile_target[:, 1]
    block_col = tile_target[:, 2]
    target = (tile_target[:, 0] * 4 + block_row // 32) * 8 + block_col // 16
    spot = (block_row % 32) * 16 + block_col % 16
    number = jnp.arange(HELD)
    same = target[:, None] == target[None, :]
    rank = jnp.sum((same & (number[None, :] < number[:, None])).astype(jnp.int32), axis=1)
    key = 2 * target + rank
    hit = key[None, :] == jnp.arange(2 * DEV)[:, None]
    idx = jnp.sum(jnp.where(hit, number[None, :], 0), axis=1)
    place = jnp.sum(jnp.where(hit, spot[None, :] + 1, 0), axis=1) - 1
    place = place.astype(F32).reshape(DEV, 2)
    return idx, jnp.repeat(place, BLK, axis=1)


def on_device(base_front, child_tiles, tile_target, fill_pattern):
    idx, meta = slots(tile_target)
    recv, l, lc = exchange(idx, meta, child_tiles, base_front)
    front_out, factor = update(base_front, recv, l, lc, fill_pattern)
    return front_out, factor


def solution(mesh):
    in_specs = (
        P("front", "prow", "pcol"),
        P(("front", "prow", "pcol"), None),
        P(("front", "prow", "pcol"), None),
        P("front", "prow", "pcol"),
    )
    out_specs = (P("front", "prow", "pcol"), P("front", "prow", None))
    return jax.shard_map(
        on_device, mesh=mesh, in_specs=in_specs, out_specs=out_specs, check_vma=False
    )
```

profile of v0, /device:TPU:112, one launch (start us, length us, event | category | flops | bytes accessed | tf_op | source)
XLA Modules:
  0.0 183.0 jit_solution(17137313348708858287)
XLA Ops:
  0.6 0.8 add_bitcast_fusion
  1.4 0.8 fusion.4
  2.2 0.2 convert_reduce_fusion
  2.4 0.2 select_reduce_fusion
  2.6 0.8 copy.12.fill_ref
  3.4 0.1 convert_element_type.12
  3.5 0.1 copy.10
  3.6 0.1 copy.11.meta_ref
  3.7 0.0 copy-start.1
  3.7 1.6 copy-done.1
  5.3 154.5 %shard_map.59 = (f32[128,72,128]{2,1,0:T(8,128)}, f32[2048,256]{1,0:T(8,128)S(1)}, f32[1024,256]{1,0:T(8,128)S(1)}) custom-call(s32[256]{0:T(256)S(1)} %get-tuple-element.9.idx_ref, f32[128,128]{1,0:T(8,128)S(1)} %copy.11.meta_ref, f32[128,4096]{1,0:T(8,128)S(1)} %copy-done.1, f32[1,2048,1024]{2,1,0:T(8,128)} %base_ref.3), custom_call_target="tpu_custom_call" | custom-call | tf_op jit(solution)/shard_map/pallas_call | solution.py:496
  159.9 0.0 copy-start
  159.9 2.3 %copy-done = f32[128,72,128]{2,1,0:T(8,128)S(1)} copy-done((f32[128,72,128]{2,1,0:T(8,128)S(1)}, f32[128,72,128]{2,1,0:T(8,128)}, u32[]{:S(2)}) %copy-start) | copy-done | bytes 4718616
  162.2 20.8 %shard_map.60 = (f32[1,2048,1024]{2,1,0:T(8,128)}, f32[1,2048,256]{2,1,0:T(8,128)}) custom-call(f32[1,2048,1024]{2,1,0:T(8,128)} %base_ref.3, f32[128,72,128]{2,1,0:T(8,128)S(1)} %copy-done, f32[2048,256]{1,0:T(8,128)S(1)} %get-tuple-element.6.l_ref, f32[1024,256]{1,0:T(8,128)S(1)} %get-tuple-element.7.lc_ref, s32[1,32,16]{2,1,0:T(8,128)S(1)} %copy.12.fill_ref), custom_call_target="tpu_custom_call" | custom-call | tf_op jit(solution)/shard_map/pallas_call | solution.py:633
  (3 shorter events, 0.0 us)
Async XLA Ops:
  3.7 1.6 copy-start.1
  159.9 2.3 %copy-start = (f32[128,72,128]{2,1,0:T(8,128)S(1)}, f32[128,72,128]{2,1,0:T(8,128)}, u32[]{:S(2)}) copy-start(f32[128,72,128]{2,1,0:T(8,128)} %get-tuple-element.5.recv_ref) | copy-start | bytes 14155780
where the time goes:
time: 183 us
  Pallas kernels  175 us (96%)
  local copies, waits for them, and re-layouts  5.01 us (3%)
  other arithmetic  1.95 us (1%)
    pallas_call x1, Pallas kernels, exchange(): pl.pallas_call(exchange_kernel, out_shape=(jax.ShapeDtypeStruct((DEV, SLO...  155 us
    pallas_call x1, Pallas kernels, update(): pl.pallas_call(update_kernel, out_shape=(jax.ShapeDtypeStruct((1, ROWS, C...  20.8 us
    unnamed x5, local copies, waits for them, and re-layouts  4.69 us

commit v1 on v0

--- a/solution.py
+++ b/solution.py
@@ -15,7 +15,10 @@
 SENT = 65
 CHUNK = 128
 NCH = 8
-LAG = 2
+HOP = 2
+EARLY = 104
+EARLY0 = 64
+
 MESH = pl.DeviceIdType.MESH
 F32 = jnp.float32
 BF16 = jnp.bfloat16
@@ -25,6 +28,11 @@
 def split2(x):
     hi = x.astype(BF16)
     return hi, (x - hi.astype(F32)).astype(BF16)
+
+
+def split3(x):
+    hi, mid = split2(x)
+    return hi, mid, (x - hi.astype(F32) - mid.astype(F32)).astype(BF16)
 
 
 def dot_nt(a, b):
@@ -48,6 +56,29 @@
         return carry
 
     lax.fori_loop(0, HELD // 8, group, 0)
+
+
+def slots(target_ref, meta, order, idx_v):
+    t = target_ref[...]
+    target = (t[:, 0:1] * 4 + t[:, 1:2] // 32) * 8 + t[:, 2:3] // 16
+    spot = lax.rem(t[:, 1:2], 32) * 16 + lax.rem(t[:, 2:3], 16)
+    wide = jnp.broadcast_to(target, (DEV, HELD))
+    row = lax.broadcasted_iota(jnp.int32, (HELD, HELD), 0)
+    col = lax.broadcasted_iota(jnp.int32, (HELD, HELD), 1)
+    rank = jnp.sum(jnp.where((wide == wide.T) & (col < row), 1, 0), axis=1, keepdims=True)
+    here = jnp.broadcast_to(target, (HELD, DEV)) == col
+    spots = jnp.broadcast_to(spot, (HELD, DEV)) + 1
+    places = []
+    for u in range(2):
+        hit = here & (jnp.broadcast_to(rank, (HELD, DEV)) == u)
+        chosen = jnp.sum(jnp.where(hit, row, 0), axis=0, keepdims=True)
+        idx_v[u : u + 1, :] = jnp.clip(chosen, 0, HELD - 1)
+        place = jnp.sum(jnp.where(hit, spots, 0), axis=0, keepdims=True) - 1
+        places.append(jnp.broadcast_to(place.astype(F32), (BLK, DEV)))
+    meta[...] = jnp.concatenate(places, axis=0).T
+    to_scalar = pltpu.make_async_copy(idx_v, order[0], order[1])
+    to_scalar.start()
+    to_scalar.wait()
 
 
 def half_inverse(a, aw, ew):
@@ -145,9 +176,8 @@
             second = jnp.where(low, pltpu.roll(x0, 64, 1), x1)
             sides.append(jnp.concatenate([first, second], axis=0))
         x = jnp.concatenate(sides, axis=1)
-        hi, lo = split2(x)
-        lo2 = (x - hi.astype(F32) - lo.astype(F32)).astype(BF16)
-        y = dot_nn(hot, hi) + dot_nn(hot, lo) + dot_nn(hot, lo2)
+        hi, mid, lo = split3(x)
+        y = dot_nn(hot, hi) + dot_nn(hot, mid) + dot_nn(hot, lo)
         for u in range(2):
             part = y[:, u * 128 : (u + 1) * 128]
             for b in range(2):
@@ -164,13 +194,16 @@
 
 
 def exchange_kernel(
-    idx_ref,
-    meta_ref,
-    child_ref,
+    target_ref,
+    child_hbm,
     base_ref,
     recv_ref,
     l_ref,
     lc_ref,
+    idx_ref,
+    idx_v,
+    meta_ref,
+    child_ref,
     tall,
     out,
     recv_v,
@@ -180,7 +213,8 @@
     inv_t,
     aw,
     ew,
-    lchunk,
+    ms,
+    lv,
     tile_send,
     tile_recv,
     lead_send,
@@ -203,6 +237,8 @@
     def where_is(d):
         return (d // 32, lax.rem(d // 8, 4), lax.rem(d, 8))
 
+    child_in = pltpu.make_async_copy(child_hbm, child_ref, local.at[7])
+    child_in.start()
     barrier = pltpu.get_barrier_semaphore()
 
     def greet(k, carry):
@@ -227,6 +263,8 @@
         def _():
             lead_in.start()
 
+    slots(target_ref, meta_ref, (idx_ref, local.at[6]), idx_v)
+    child_in.wait()
     relayout_tiles(child_ref, tall.reshape(HELD * BLK, 128))
     pl.semaphore_wait(barrier, DEV - 1)
 
@@ -249,7 +287,7 @@
     low = lax.broadcasted_iota(jnp.int32, (BLK, 128), 1) < BLK
 
     def fill_slot(d):
-        out[d, 0:BLK, :] = jnp.where(low, tall[idx_ref[2 * d]], tall[idx_ref[2 * d + 1]])
+        out[d, 0:BLK, :] = jnp.where(low, tall[idx_ref[0, d]], tall[idx_ref[1, d]])
         out[d, pl.ds(BLK, 1), :] = meta_ref[pl.ds(d, 1), :]
 
     def send(tf, tr, tc):
@@ -273,13 +311,18 @@
         def _():
             send(tf, tr, 0)
 
-    def send_rest(k):
-        a = lax.rem(k, 4)
-        jk = lax.rem(k // 4, 16)
-        b = lax.rem(a + lax.rem(jk, 4), 4)
-        dz = lax.rem(a + jk // 4, 4)
+    def send_rest(q):
+        shift = jnp.where(z == 0, 0, 32)
+        far = q - shift
+        inside = (far < 0) | (far >= 96)
+        p = lax.rem(q, 32)
+        far = lax.rem(far + 128, 128)
+        a = lax.rem(q, 4)
+        b = lax.rem(a + jnp.where(inside, lax.rem(p // 4, 4), lax.rem(far // 12, 4)), 4)
+        dz = jnp.where(inside, 0, 1 + lax.rem(far, 3))
+        dh = jnp.where(inside, p // 16, far // 48)
         tf, tr = lax.rem(f + a, 4), lax.rem(r + b, 4)
-        tc = lax.rem(z + dz, 4) * 2 + lax.rem(h + k // 64, 2)
+        tc = lax.rem(z + dz, 4) * 2 + lax.rem(h + dh, 2)
 
         @pl.when((tc != 0) & ((tf != f) | (tr != r) | (tc != c)))
         def _():
@@ -287,15 +330,17 @@
 
     def phase_one(k, carry):
         send_first(k)
-        send_rest(k)
         return carry
 
     def phase_two(k, carry):
         send_rest(k)
         return carry
 
+    def send_range(lo, hi):
+        lax.fori_loop(lo, hi, phase_two, 0)
+
     lax.fori_loop(0, 16, phase_one, 0)
-    lax.fori_loop(16, DEV, phase_two, 0)
+    send_range(0, jnp.where(first_col, EARLY0, EARLY))
     fill_slot(me)
     own_tiles = pltpu.make_async_copy(
         out.at[me, pl.ds(0, SENT)], recv_ref.at[me, pl.ds(0, SENT)], local.at[3]
@@ -315,24 +360,22 @@
     def strip(k):
         return pl.ds(pl.multiple_of(k * CHUNK, CHUNK), CHUNK)
 
-    def push(rows, send_sem, recv_sem, target):
+    def push(src, half, k, send_sem, recv_sem, target):
         return pltpu.make_async_remote_copy(
-            src_ref=l_ref.at[rows],
-            dst_ref=l_ref.at[rows],
+            src_ref=src.at[piece(half, k)],
+            dst_ref=l_ref.at[piece(half, k)],
             send_sem=send_sem,
             recv_sem=recv_sem,
             device_id=target,
             device_id_type=MESH,
         )
 
-    def z_next(half, k):
+    def z_next(src, half, k):
         nz = lax.rem(z + 1 + 2 * half, 4)
-        return push(
-            piece(half, k), z_send.at[half * NCH + k], own_recv.at[k], (f, r, nz * 2 + half)
-        )
-
-    def cross(half, k, recv_sem):
-        return push(piece(half, k), c_send.at[half * NCH + k], recv_sem, (f, r, z * 2 + 1 - h))
+        return push(src, half, k, z_send.at[half * NCH + k], own_recv.at[k], (f, r, nz * 2 + half))
+
+    def cross(src, half, k, recv_sem):
+        return push(src, half, k, c_send.at[half * NCH + k], recv_sem, (f, r, z * 2 + 1 - h))
 
     def x_hop(src, k):
         nr = lax.rem(r + 1 + 2 * lax.rem(k, 2), 4)
@@ -348,24 +391,25 @@
     x_root = r == z
     x_dist = lax.rem(r - z + 4, 4)
 
-    def lc_local(k):
-        return pltpu.make_async_copy(l_ref.at[piece(h, k)], lc_ref.at[strip(k)], local.at[4])
-
     def x_forwards(k):
         return jnp.where(lax.rem(k, 2) == 0, x_dist != 3, x_dist != 1)
 
-    def x_start(k):
-        x_hop(l_ref.at[piece(h, k)], k).start()
-        own = lc_local(k)
-        own.start()
-        own.wait()
-
     def x_pass(k):
         x_hop(lc_ref.at[strip(k)], k).wait_recv()
 
         @pl.when(x_forwards(k))
         def _():
             x_hop(lc_ref.at[strip(k)], k).start()
+
+    def x_due(t):
+        for odd in range(2):
+            k = t - HOP * (4 - x_dist if odd else x_dist)
+
+            @pl.when(jnp.logical_not(x_root) & (k >= 0) & (k < NCH) & (lax.rem(k + NCH * 4, 2) == odd))
+            def _():
+                x_pass(k)
+
+    keep = pltpu.make_async_copy(lv, l_ref, local.at[4])
 
     @pl.when(first_col)
     def _():
@@ -374,6 +418,10 @@
             lead_copy(1).wait_recv()
 
         pivot_inverse(lead, inv_t, aw, ew)
+        m1, m2, m3 = split3(inv_t[...])
+        ms[0] = m1
+        ms[1] = m2
+        ms[2] = m3
         all_tiles.wait()
         panel_in0.wait()
         panel_in1.wait()
@@ -387,71 +435,70 @@
             return carry
 
         lax.fori_loop(0, DEV, fetch, 0)
-
         pltpu.make_async_copy(
             recv_ref.at[:, pl.ds(0, SENT)], recv_ref.at[:, pl.ds(0, SENT)], local.at[5]
         ).wait()
         assemble_panel(recv_v, (panel0, panel1))
 
-        def produce(k, carry):
-            for half in range(2):
-                rows = piece(half, k)
-                p = jnp.concatenate([panel0[rows, :], panel1[rows, :]], axis=1)
-                lchunk[half] = jnp.dot(p, inv_t[...], precision=HI, preferred_element_type=F32)
-                keep = pltpu.make_async_copy(lchunk.at[half], l_ref.at[rows], local.at[6])
-                keep.start()
-                keep.wait()
-                z_next(half, k).start()
-            cross(0, k, oth_recv.at[k]).start()
-            cross(1, k, own_recv.at[k]).start()
-
-            @pl.when(x_root)
+        def produce(t, carry):
+            @pl.when(t < NCH)
             def _():
-                x_start(k)
-
+                k = t
+                for half in range(2):
+                    rows = piece(half, k)
+                    p1, p2, p3 = split3(jnp.concatenate([panel0[rows, :], panel1[rows, :]], axis=1))
+                    lv[rows, :] = (
+                        dot_nn(p1, ms[0])
+                        + (dot_nn(p1, ms[1]) + dot_nn(p2, ms[0]))
+                        + (dot_nn(p1, ms[2]) + dot_nn(p2, ms[1]) + dot_nn(p3, ms[0]))
+                    )
+                    z_next(lv, half, k).start()
+                    cross(lv, half, k, (oth_recv, own_recv)[half].at[k]).start()
+
+                @pl.when(x_root)
+                def _():
+                    x_hop(lv.at[piece(0, k)], k).start()
+
+                send_range(EARLY0 + k * ((DEV - EARLY0) // NCH), EARLY0 + (k + 1) * ((DEV - EARLY0) // NCH))
+
+            x_due(t)
             return carry
 
-        lax.fori_loop(0, NCH, produce, 0)
-
-        @pl.when(r != 0)
-        def _():
-            def take(k, carry):
-                x_pass(k)
-                return carry
-
-            lax.fori_loop(0, NCH, take, 0)
+        lax.fori_loop(0, NCH + 3 * HOP, produce, 0)
+        keep.start()
+        send_range(DEV - (DEV - EARLY0) % NCH, DEV)
 
     z_forwards = ((h == 0) & ((z == 1) | (z == 2))) | ((h == 1) & ((z == 3) | (z == 2)))
 
     @pl.when(jnp.logical_not(first_col))
     def _():
-        def relay(k, carry):
-            @pl.when(k < NCH)
+        def relay(t, carry):
+            @pl.when(t < NCH)
             def _():
-                z_next(h, k).wait_recv()
+                k = t
+                z_next(l_ref, h, k).wait_recv()
 
                 @pl.when(z_forwards)
                 def _():
-                    z_next(h, k).start()
+                    z_next(l_ref, h, k).start()
+
+                @pl.when(x_root)
+                def _():
+                    x_hop(l_ref.at[piece(h, k)], k).start()
 
                 @pl.when(z != 0)
                 def _():
-                    cross(h, k, oth_recv.at[k]).start()
-
-                @pl.when(x_root)
-                def _():
-                    x_start(k)
-
-            @pl.when((k >= LAG) & jnp.logical_not(x_root))
-            def _():
-                x_pass(k - LAG)
-
+                    cross(l_ref, h, k, oth_recv.at[k]).start()
+
+                send_range(EARLY + k * ((DEV - EARLY) // NCH), EARLY + (k + 1) * ((DEV - EARLY) // NCH))
+
+            x_due(t)
             return carry
 
-        lax.fori_loop(0, NCH + LAG, relay, 0)
+        lax.fori_loop(0, NCH + 3 * HOP, relay, 0)
 
         def other(k, carry):
-            cross(1 - h, k, oth_recv.at[k]).wait_recv()
+            cross(l_ref, 1 - h, k, oth_recv.at[k]).wait_recv()
             return carry
 
         lax.fori_loop(0, NCH, other, 0)
@@ -463,25 +510,29 @@
         tile_send,
     ).wait()
 
-    @pl.when(first_col & (r == 0))
+    @pl.when(first_col)
     def _():
-        for j in range(1, 4):
-            lead_copy(j).wait_send()
+        keep.wait()
+
+        @pl.when(r == 0)
+        def _():
+            for j in range(1, 4):
+                lead_copy(j).wait_send()
 
     def drain(k, carry):
         @pl.when(first_col)
         def _():
             for half in range(2):
-                z_next(half, k).wait_send()
-                cross(half, k, own_recv.at[k]).wait_send()
+                z_next(lv, half, k).wait_send()
+                cross(lv, half, k, own_recv.at[k]).wait_send()
 
         @pl.when(z_forwards)
         def _():
-            z_next(h, k).wait_send()
+            z_next(l_ref, h, k).wait_send()
 
         @pl.when(z != 0)
         def _():
-            cross(h, k, own_recv.at[k]).wait_send()
+            cross(l_ref, h, k, own_recv.at[k]).wait_send()
 
         @pl.when(x_root | x_forwards(k))
         def _():
@@ -492,7 +543,7 @@
     lax.fori_loop(0, NCH, drain, 0)
 
 
-def exchange(idx, meta, child_tiles, base_front):
+def exchange(tile_target, child_tiles, base_front):
     return pl.pallas_call(
         exchange_kernel,
         out_shape=(
@@ -501,9 +552,8 @@
             jax.ShapeDtypeStruct((COLS, PW), F32),
         ),
         in_specs=[
-            pl.BlockSpec(memory_space=pltpu.SMEM),
             pl.BlockSpec(memory_space=pltpu.VMEM),
-            pl.BlockSpec(memory_space=pltpu.VMEM),
+            pl.BlockSpec(memory_space=pl.ANY),
             pl.BlockSpec(memory_space=pl.ANY),
         ],
         out_specs=(
@@ -512,6 +562,10 @@
             pl.BlockSpec(memory_space=pl.ANY),
         ),
         scratch_shapes=[
+            pltpu.SMEM((2, DEV), jnp.int32),
+            pltpu.VMEM((2, DEV), jnp.int32),
+            pltpu.VMEM((DEV, 128), F32),
+            pltpu.VMEM((HELD, BLK * BLK), F32),
             pltpu.VMEM((HELD, BLK, 128), F32),
             pltpu.VMEM((DEV, SLOT, 128), F32),
             pltpu.VMEM((DEV * SLOT, 128), F32),
@@ -521,7 +575,8 @@
             pltpu.VMEM((PW, PW), F32),
             pltpu.VMEM((128, 128), F32),
             pltpu.VMEM((128, 128), F32),
-            pltpu.VMEM((2, CHUNK, PW), F32),
+            pltpu.VMEM((3, PW, PW), BF16),
+            pltpu.VMEM((ROWS, PW), F32),
             pltpu.SemaphoreType.DMA(()),
             pltpu.SemaphoreType.DMA(()),
             pltpu.SemaphoreType.DMA((3,)),
@@ -535,20 +590,21 @@
             pltpu.SemaphoreType.DMA((8,)),
         ],
         compiler_params=pltpu.CompilerParams(
-            collective_id=0, has_side_effects=True, vmem_limit_bytes=48 << 20
+            collective_id=0, has_side_effects=True, vmem_limit_bytes=56 << 20
         ),
-    )(idx, meta, child_tiles, base_front)
+    )(tile_target, child_tiles, base_front)
 
 
 STEP = 256
+STEPS = ROWS // STEP
 
 
 def update_kernel(
-    base_ref, recv_ref, l_ref, lc_ref, fill_ref, front_ref, factor_ref, acc, tiles, lv, lcv, lc_hi, lc_lo, keep, place, base_in, out_sem, sems
+    base_ref, recv_ref, l_ref, lc_ref, fill_ref, front_ref, factor_ref,
+    acc, tiles, lv, lcv, lc_hi, lc_lo, keep, place, todo, count, base_in, out_sem, sems
 ):
     r = lax.axis_index("prow")
     c = lax.axis_index("pcol")
-    steps = ROWS // STEP
 
     def strip(i):
         return pl.ds(pl.multiple_of(i * STEP, STEP), STEP)
@@ -559,18 +615,30 @@
     def store(i):
         return pltpu.make_async_copy(acc.at[strip(i)], front_ref.at[0, strip(i)], out_sem.at[i])
 
+    z = c // 2
+    own_rows = pl.ds(pl.multiple_of(lax.rem(c, 2) * COLS, COLS), COLS)
     l_in = pltpu.make_async_copy(l_ref, lv, sems.at[0])
     lc_in = pltpu.make_async_copy(lc_ref, lcv, sems.at[1])
+    lc_own = pltpu.make_async_copy(l_ref.at[own_rows], lcv, sems.at[1])
     tiles_in = pltpu.make_async_copy(
-        recv_ref.at[:, pl.ds(0, BLK)], tiles, sems.at[2]
+        recv_ref.at[:, pl.ds(0, BLK)], tiles.at[pl.ds(0, DEV)], sems.at[2]
     )
     place_in = pltpu.make_async_copy(recv_ref.at[:, BLK], place, sems.at[3])
-    lc_in.start()
+    place_in.start()
+
+    @pl.when(r == z)
+    def _():
+        lc_own.start()
+
+    @pl.when(r != z)
+    def _():
+        lc_in.start()
+
+    load(0).start()
+    tiles_in.start()
     l_in.start()
-    for i in range(steps):
+    for i in range(1, STEPS):
         load(i).start()
-    place_in.start()
-    tiles_in.start()
     row_block = lax.broadcasted_iota(jnp.int32, (32, 16), 0) + 32 * r
     col_block = lax.broadcasted_iota(jnp.int32, (32, 16), 1) + 16 * c
     on = (fill_ref[0] > 0) & (row_block >= PW // BLK) & (col_block >= PW // BLK)
@@ -579,15 +647,44 @@
         == lax.broadcasted_iota(jnp.int32, (16, COLS), 0)
     ).astype(BF16)
     keep[...] = dot_nn(on.astype(BF16), spread)
+
+    for i in range(STEPS):
+        count[i] = 0
+    place_in.wait()
+
+    def sort(s, carry):
+        for u in range(2):
+            p = place[s, u * BLK].astype(jnp.int32)
+
+            @pl.when(p >= 0)
+            def _():
+                i = lax.shift_right_logical(p, 6)
+                n = count[i]
+                source = s + DEV * jnp.bitwise_and(p + u, 1)
+                todo[i * 2 * DEV + n] = source * 512 + p
+                count[i] = n + 1
+
+        return carry
+
+    lax.fori_loop(0, DEV, sort, 0)
     lc_in.wait()
     hi, lo = split2(lcv[...])
     lc_hi[...] = hi
     lc_lo[...] = lo
+    tiles_in.wait()
+
+    def swap(s, carry):
+        for u in range(4):
+            tiles[DEV + 4 * s + u] = pltpu.roll(tiles[4 * s + u], 64, 1)
+        return carry
+
+    lax.fori_loop(0, DEV // 4, swap, 0)
     l_in.wait()
     factor_out = pltpu.make_async_copy(lv, factor_ref.at[0], sems.at[4])
     factor_out.start()
-
-    def product(i, carry):
+    half = lax.broadcasted_iota(jnp.int32, (BLK, 128), 1) // BLK
+
+    def rows_of(i, carry):
         load(i).wait()
         a_hi, a_lo = split2(lv[strip(i), :])
         p = dot_nt(a_hi, lc_hi[...]) + dot_nt(a_hi, lc_lo[...]) + dot_nt(a_lo, lc_hi[...])
@@ -595,37 +692,26 @@
             rows = pl.ds(pl.multiple_of(i * STEP + b * BLK, BLK), BLK)
             mask = jnp.broadcast_to(keep[pl.ds(i * (STEP // BLK) + b, 1), :], (BLK, COLS))
             acc[rows, :] = acc[rows, :] - p[b * BLK : (b + 1) * BLK, :] * mask
-        return carry
-
-    lax.fori_loop(0, steps, product, 0)
-    place_in.wait()
-    tiles_in.wait()
-    half = lax.broadcasted_iota(jnp.int32, (BLK, 128), 1) // BLK
-
-    def add(s, carry):
-        for u in range(2):
-            p = place[s, u * BLK].astype(jnp.int32)
-
-            @pl.when(p >= 0)
-            def _():
-                rb = lax.shift_right_logical(p, 4)
-                cb = jnp.bitwise_and(p, 15)
-                side = jnp.bitwise_and(cb, 1)
-                t = tiles[s]
-                moved = pltpu.roll(t, 64, 1)
-                v = jnp.where(side == u, t, moved)
-                v = jnp.where(half == side, v, 0.0)
-                rows = pl.ds(pl.multiple_of(rb * BLK, BLK), BLK)
-                cols = pl.ds(pl.multiple_of(lax.shift_right_logical(cb, 1) * 128, 128), 128)
-                acc[rows, cols] = acc[rows, cols] + v
-
-        return carry
-
-    lax.fori_loop(0, DEV, add, 0)
-    for i in range(steps):
+
+        def add(n, carry):
+            e = todo[i * 2 * DEV + n]
+            rb = jnp.bitwise_and(lax.shift_right_logical(e, 4), 31)
+            cb = jnp.bitwise_and(lax.shift_right_logical(e, 1), 7)
+            v = jnp.where(half == jnp.bitwise_and(e, 1), tiles[lax.shift_right_logical(e, 9)], 0.0)
+            at = (
+                pl.ds(pl.multiple_of(rb * BLK, BLK), BLK),
+                pl.ds(pl.multiple_of(cb * 128, 128), 128),
+            )
+            acc[at] = acc[at] + v
+            return carry
+
+        lax.fori_loop(0, count[i], add, 0)
         store(i).start()
+        return carry
+
+    lax.fori_loop(0, STEPS, rows_of, 0)
     factor_out.wait()
-    for i in range(steps):
+    for i in range(STEPS):
         store(i).wait()
 
 
@@ -641,40 +727,25 @@
         out_specs=(pl.BlockSpec(memory_space=pl.ANY), pl.BlockSpec(memory_space=pl.ANY)),
         scratch_shapes=[
             pltpu.VMEM((ROWS, COLS), F32),
-            pltpu.VMEM((DEV, BLK, 128), F32),
+            pltpu.VMEM((2 * DEV, BLK, 128), F32),
             pltpu.VMEM((ROWS, PW), F32),
             pltpu.VMEM((COLS, PW), F32),
             pltpu.VMEM((COLS, PW), BF16),
             pltpu.VMEM((COLS, PW), BF16),
             pltpu.VMEM((32, COLS), F32),
             pltpu.SMEM((DEV, 128), F32),
-            pltpu.SemaphoreType.DMA((ROWS // STEP,)),
-            pltpu.SemaphoreType.DMA((ROWS // STEP,)),
+            pltpu.SMEM((STEPS * 2 * DEV,), jnp.int32),
+            pltpu.SMEM((STEPS,), jnp.int32),
+            pltpu.SemaphoreType.DMA((STEPS,)),
+            pltpu.SemaphoreType.DMA((STEPS,)),
             pltpu.SemaphoreType.DMA((5,)),
         ],
-        compiler_params=pltpu.CompilerParams(vmem_limit_bytes=40 << 20),
+        compiler_params=pltpu.CompilerParams(vmem_limit_bytes=58 << 20),
     )(base_front, recv, l, lc, fill_pattern)
 
 
-def slots(tile_target):
-    block_row = tile_target[:, 1]
-    block_col = tile_target[:, 2]
-    target = (tile_target[:, 0] * 4 + block_row // 32) * 8 + block_col // 16
-    spot = (block_row % 32) * 16 + block_col % 16
-    number = jnp.arange(HELD)
-    same = target[:, None] == target[None, :]
-    rank = jnp.sum((same & (number[None, :] < number[:, None])).astype(jnp.int32), axis=1)
-    key = 2 * target + rank
-    hit = key[None, :] == jnp.arange(2 * DEV)[:, None]
-    idx = jnp.sum(jnp.where(hit, number[None, :], 0), axis=1)
-    place = jnp.sum(jnp.where(hit, spot[None, :] + 1, 0), axis=1) - 1
-    place = place.astype(F32).reshape(DEV, 2)
-    return idx, jnp.repeat(place, BLK, axis=1)
-
-
 def on_device(base_front, child_tiles, tile_target, fill_pattern):
-    idx, meta = slots(tile_target)
-    recv, l, lc = exchange(idx, meta, child_tiles, base_front)
+    recv, l, lc = exchange(tile_target, child_tiles, base_front)
     front_out, factor = update(base_front, recv, l, lc, fill_pattern)
     return front_out, factor
 

time: 183 us -> 125 us (0.68)
  the two profiles are of different devices: /device:TPU:112 before, /device:TPU:37 now
where the time goes in v1:
time: 125 us; the launch traced here: 124 us
  Pallas kernels  121 us (97%)
  local copies, waits for them, and re-layouts  2.79 us (2%)
    pallas_call x1, Pallas kernels, exchange(): pl.pallas_call(exchange_kernel, out_shape=(jax.ShapeDtypeStruct((DEV, SLO...  104 us
    pallas_call x1, Pallas kernels, update(): pl.pallas_call(update_kernel, out_shape=(jax.ShapeDtypeStruct((1, ROWS, C...  16.7 us
    unnamed x2, local copies, waits for them, and re-layouts  2.79 us

profile of v1, /device:TPU:37, one launch (start us, length us, event | category | flops | bytes accessed | tf_op | source)
XLA Modules:
  0.0 124.2 jit_solution(3762314990805857404)
XLA Ops:
  0.6 1.4 %copy.7.fill_ref = s32[1,32,16]{2,1,0:T(8,128)} copy(s32[1,32,16]{1,2,0:T(8,128)} %param.7) | data formatting | bytes 4096 | tf_op args[3]
  2.0 1.4 %copy.6.target_ref = s32[128,3]{1,0:T(8,128)} copy(s32[128,3]{0,1:T(4,128)} %param.6) | data formatting | bytes 3072 | tf_op args[2]
  3.4 104.1 %shard_map.59 = (f32[128,72,128]{2,1,0:T(8,128)}, f32[2048,256]{1,0:T(8,128)}, f32[1024,256]{1,0:T(8,128)}) custom-call(s32[128,3]{1,0:T(8,128)} %copy.6.target_ref, f32[128,4096]{1,0:T(8,128)} %child_hbm.1, f32[1,2048,1024]{2,1,0:T(8,128)} %base_ref.3), custom_call_target="tpu_custom_call" | custom-call | tf_op jit(solution)/shard_map/pallas_call | solution.py:547
  107.5 16.7 %shard_map.60 = (f32[1,2048,1024]{2,1,0:T(8,128)}, f32[1,2048,256]{2,1,0:T(8,128)}) custom-call(f32[1,2048,1024]{2,1,0:T(8,128)} %base_ref.3, f32[128,72,128]{2,1,0:T(8,128)} %get-tuple-element.5.recv_ref, f32[2048,256]{1,0:T(8,128)} %get-tuple-element.6.l_ref, f32[1024,256]{1,0:T(8,128)} %get-tuple-element.7.lc_ref, s32[1,32,16]{2,1,0:T(8,128)} %copy.7.fill_ref), custom_call_target="tpu_custom_call" | custom-call | tf_op jit(solution)/shard_map/pallas_call | solution.py:719

commit v2 on v1

--- a/solution.py
+++ b/solution.py
@@ -15,9 +15,7 @@
 SENT = 65
 CHUNK = 128
 NCH = 8
-HOP = 2
-EARLY = 104
-EARLY0 = 64
+HOP = 3
 
 MESH = pl.DeviceIdType.MESH
 F32 = jnp.float32
@@ -28,11 +26,6 @@
 def split2(x):
     hi = x.astype(BF16)
     return hi, (x - hi.astype(F32)).astype(BF16)
-
-
-def split3(x):
-    hi, mid = split2(x)
-    return hi, mid, (x - hi.astype(F32) - mid.astype(F32)).astype(BF16)
 
 
 def dot_nt(a, b):
@@ -152,52 +145,45 @@
     inv_t[128:256, 0:128] = jnp.zeros((128, 128), F32)
 
 
-def assemble_panel(recv_v, panels):
-    lane = lax.broadcasted_iota(jnp.int32, (128, 128), 1)
-    low = lane < BLK
+def mark_places(recv, hot):
+    place = recv[pl.ds(BLK, DEV, stride=SLOT), :].T
+    row = lax.broadcasted_iota(jnp.int32, (512, 128), 0)
+    want = (lax.rem(row, 32) * 16 + row // 32).astype(F32)
+    for u in range(2):
+        there = jnp.broadcast_to(place[u * BLK : u * BLK + 1, :], (512, 128))
+        hot[:, u * 128 : (u + 1) * 128] = (want == there).astype(BF16)
+
+
+def add_rows(i, recv, hot, strips):
+    low = lax.broadcasted_iota(jnp.int32, (128, 128), 1) < BLK
     low32 = lax.broadcasted_iota(jnp.int32, (32, 128), 1) < BLK
-    place = recv_v[pl.ds(BLK, DEV, stride=SLOT), :].T
-    row = lax.broadcasted_iota(jnp.int32, (128, 128), 0)
-    want = (lax.rem(row, 32) * 16 + row // 32).astype(F32)
-    hot = jnp.concatenate(
-        [
-            (want == jnp.broadcast_to(place[0:1, :], (128, 128))).astype(BF16),
-            (want == jnp.broadcast_to(place[BLK : BLK + 1, :], (128, 128))).astype(BF16),
-        ],
-        axis=1,
-    )
-
-    def quad(i, carry):
-        sides = []
-        for u in range(2):
-            x0 = recv_v[pl.ds(4 * i + 2 * u, DEV, stride=SLOT), :]
-            x1 = recv_v[pl.ds(4 * i + 2 * u + 1, DEV, stride=SLOT), :]
-            first = jnp.where(low, x0, pltpu.roll(x1, 64, 1))
-            second = jnp.where(low, pltpu.roll(x0, 64, 1), x1)
-            sides.append(jnp.concatenate([first, second], axis=0))
-        x = jnp.concatenate(sides, axis=1)
-        hi, mid, lo = split3(x)
-        y = dot_nn(hot, hi) + dot_nn(hot, mid) + dot_nn(hot, lo)
-        for u in range(2):
-            part = y[:, u * 128 : (u + 1) * 128]
-            for b in range(2):
-                even = part[b * 64 : b * 64 + 32, :]
-                odd = part[b * 64 + 32 : b * 64 + 64, :]
-                add0 = jnp.where(low32, even, pltpu.roll(odd, 64, 1))
-                add1 = jnp.where(low32, pltpu.roll(even, 64, 1), odd)
-                for v, add in ((0, add0), (1, add1)):
-                    rows = pl.ds(4 * i + 2 * u + v, 32, stride=BLK)
-                    panels[b][rows, :] = panels[b][rows, :] + add
-        return carry
-
-    lax.fori_loop(0, 16, quad, 0)
+    sides = []
+    for u in range(2):
+        x0 = recv[pl.ds(4 * i + 2 * u, DEV, stride=SLOT), :]
+        x1 = recv[pl.ds(4 * i + 2 * u + 1, DEV, stride=SLOT), :]
+        first = jnp.where(low, x0, pltpu.roll(x1, 64, 1))
+        second = jnp.where(low, pltpu.roll(x0, 64, 1), x1)
+        sides.append(jnp.concatenate([first, second], axis=0))
+    hi, lo = split2(jnp.concatenate(sides, axis=1))
+    mark = hot[0 : 64 * len(strips), :]
+    y = dot_nn(mark, hi) + dot_nn(mark, lo)
+    for u in range(2):
+        part = y[:, u * 128 : (u + 1) * 128]
+        for b, strip in enumerate(strips):
+            even = part[b * 64 : b * 64 + 32, :]
+            odd = part[b * 64 + 32 : b * 64 + 64, :]
+            add0 = jnp.where(low32, even, pltpu.roll(odd, 64, 1))
+            add1 = jnp.where(low32, pltpu.roll(even, 64, 1), odd)
+            for v, add in ((0, add0), (1, add1)):
+                rows = pl.ds(4 * i + 2 * u + v, 32, stride=BLK)
+                strip[rows, :] = strip[rows, :] + add
 
 
 def exchange_kernel(
     target_ref,
     child_hbm,
     base_ref,
-    recv_ref,
+    sum_ref,
     l_ref,
     lc_ref,
     idx_ref,
@@ -206,7 +192,9 @@
     child_ref,
     tall,
     out,
-    recv_v,
+    recv_ref,
+    acc,
+    hot,
     panel0,
     panel1,
     lead,
@@ -237,6 +225,10 @@
     def where_is(d):
         return (d // 32, lax.rem(d // 8, 4), lax.rem(d, 8))
 
+    for b in range(COLS // 128):
+        pltpu.make_async_copy(
+            base_ref.at[0, :, pl.ds(b * 128, 128)], acc.at[b], local.at[8]
+        ).start()
     child_in = pltpu.make_async_copy(child_hbm, child_ref, local.at[7])
     child_in.start()
     barrier = pltpu.get_barrier_semaphore()
@@ -302,45 +294,23 @@
             device_id_type=MESH,
         ).start()
 
-    def send_first(k):
+    def send_to(k):
         a = lax.rem(k, 4)
-        b = lax.rem(a + k // 4, 4)
+        jk = lax.rem(k // 4, 16)
+        b = lax.rem(a + lax.rem(jk, 4), 4)
+        dz = lax.rem(a + jk // 4, 4)
         tf, tr = lax.rem(f + a, 4), lax.rem(r + b, 4)
-
-        @pl.when((tf != f) | (tr != r) | (c != 0))
-        def _():
-            send(tf, tr, 0)
-
-    def send_rest(q):
-        shift = jnp.where(z == 0, 0, 32)
-        far = q - shift
-        inside = (far < 0) | (far >= 96)
-        p = lax.rem(q, 32)
-        far = lax.rem(far + 128, 128)
-        a = lax.rem(q, 4)
-        b = lax.rem(a + jnp.where(inside, lax.rem(p // 4, 4), lax.rem(far // 12, 4)), 4)
-        dz = jnp.where(inside, 0, 1 + lax.rem(far, 3))
-        dh = jnp.where(inside, p // 16, far // 48)
-        tf, tr = lax.rem(f + a, 4), lax.rem(r + b, 4)
-        tc = lax.rem(z + dz, 4) * 2 + lax.rem(h + dh, 2)
-
-        @pl.when((tc != 0) & ((tf != f) | (tr != r) | (tc != c)))
+        tc = lax.rem(z + dz, 4) * 2 + lax.rem(h + k // 64, 2)
+
+        @pl.when((tf != f) | (tr != r) | (tc != c))
         def _():
             send(tf, tr, tc)
 
-    def phase_one(k, carry):
-        send_first(k)
+    def send_step(k, carry):
+        send_to(k)
         return carry
 
-    def phase_two(k, carry):
-        send_rest(k)
-        return carry
-
-    def send_range(lo, hi):
-        lax.fori_loop(lo, hi, phase_two, 0)
-
-    lax.fori_loop(0, 16, phase_one, 0)
-    send_range(0, jnp.where(first_col, EARLY0, EARLY))
+    lax.fori_loop(0, DEV, send_step, 0)
     fill_slot(me)
     own_tiles = pltpu.make_async_copy(
         out.at[me, pl.ds(0, SENT)], recv_ref.at[me, pl.ds(0, SENT)], local.at[3]
@@ -410,6 +380,10 @@
                 x_pass(k)
 
     keep = pltpu.make_async_copy(lv, l_ref, local.at[4])
+    recv = recv_ref.reshape(DEV * SLOT, 128)
+    strips = [acc.at[b] for b in range(COLS // 128)]
+    whole_in = pltpu.make_async_copy(acc, acc, local.at[8])
+    whole_out = pltpu.make_async_copy(acc, sum_ref, local.at[5])
 
     @pl.when(first_col)
     def _():
@@ -418,60 +392,75 @@
             lead_copy(1).wait_recv()
 
         pivot_inverse(lead, inv_t, aw, ew)
-        m1, m2, m3 = split3(inv_t[...])
-        ms[0] = m1
-        ms[1] = m2
-        ms[2] = m3
+        m_hi, m_lo = split2(inv_t[...])
+        ms[0] = m_hi
+        ms[1] = m_lo
         all_tiles.wait()
         panel_in0.wait()
         panel_in1.wait()
 
-        def fetch(i, carry):
-            pltpu.make_async_copy(
-                recv_ref.at[i, pl.ds(0, SENT)],
-                recv_v.at[pl.ds(pl.multiple_of(i * SLOT, 8), SENT)],
-                local.at[5],
-            ).start()
+        mark_places(recv, hot)
+
+        def panel_rows(i, carry):
+            add_rows(i, recv, hot, (panel0, panel1))
             return carry
 
-        lax.fori_loop(0, DEV, fetch, 0)
-        pltpu.make_async_copy(
-            recv_ref.at[:, pl.ds(0, SENT)], recv_ref.at[:, pl.ds(0, SENT)], local.at[5]
-        ).wait()
-        assemble_panel(recv_v, (panel0, panel1))
-
-        def produce(t, carry):
-            @pl.when(t < NCH)
+        lax.fori_loop(0, BLK // 4, panel_rows, 0)
+
+        def produce(k, carry):
+            top, bottom = piece(0, k), piece(1, k)
+            p = jnp.concatenate(
+                [
+                    jnp.concatenate([panel0[top, :], panel0[bottom, :]], axis=0),
+                    jnp.concatenate([panel1[top, :], panel1[bottom, :]], axis=0),
+                ],
+                axis=1,
+            )
+            p_hi, p_lo = split2(p)
+            y = dot_nn(p_hi, ms[0]) + dot_nn(p_hi, ms[1]) + dot_nn(p_lo, ms[0])
+            lv[top, :] = y[:CHUNK]
+            lv[bottom, :] = y[CHUNK:]
+            for half in range(2):
+                z_next(lv, half, k).start()
+                cross(lv, half, k, (oth_recv, own_recv)[half].at[k]).start()
+
+            @pl.when(x_root)
             def _():
-                k = t
-                for half in range(2):
-                    rows = piece(half, k)
-                    p1, p2, p3 = split3(jnp.concatenate([panel0[rows, :], panel1[rows, :]], axis=1))
-                    lv[rows, :] = (
-                        dot_nn(p1, ms[0])
-                        + (dot_nn(p1, ms[1]) + dot_nn(p2, ms[0]))
-                        + (dot_nn(p1, ms[2]) + dot_nn(p2, ms[1]) + dot_nn(p3, ms[0]))
-                    )
-                    z_next(lv, half, k).start()
-                    cross(lv, half, k, (oth_recv, own_recv)[half].at[k]).start()
-
-                @pl.when(x_root)
-                def _():
-                    x_hop(lv.at[piece(0, k)], k).start()
-
-                send_range(EARLY0 + k * ((DEV - EARLY0) // NCH), EARLY0 + (k + 1) * ((DEV - EARLY0) // NCH))
-
+                x_hop(lv.at[piece(0, k)], k).start()
+
+            return carry
+
+        lax.fori_loop(0, NCH, produce, 0)
+        keep.start()
+        whole_in.wait()
+
+        def own_rows(t, carry):
             x_due(t)
+
+            @pl.when(t < BLK // 4)
+            def _():
+                add_rows(t, recv, hot, strips)
+
             return carry
 
-        lax.fori_loop(0, NCH + 3 * HOP, produce, 0)
-        keep.start()
-        send_range(DEV - (DEV - EARLY0) % NCH, DEV)
+        lax.fori_loop(0, max(BLK // 4, NCH + 3 * HOP), own_rows, 0)
+        whole_out.start()
 
     z_forwards = ((h == 0) & ((z == 1) | (z == 2))) | ((h == 1) & ((z == 3) | (z == 2)))
 
     @pl.when(jnp.logical_not(first_col))
     def _():
+        all_tiles.wait()
+        whole_in.wait()
+        mark_places(recv, hot)
+
+        def own_rows(i, carry):
+            add_rows(i, recv, hot, strips)
+            return carry
+
+        lax.fori_loop(0, BLK // 4, own_rows, 0)
+        whole_out.start()
+
         def relay(t, carry):
             @pl.when(t < NCH)
             def _():
@@ -490,8 +479,6 @@
                 def _():
                     cross(l_ref, h, k, oth_recv.at[k]).start()
 
-                send_range(EARLY + k * ((DEV - EARLY) // NCH), EARLY + (k + 1) * ((DEV - EARLY) // NCH))
-
             x_due(t)
             return carry
 
@@ -502,8 +489,8 @@
             return carry
 
         lax.fori_loop(0, NCH, other, 0)
-        all_tiles.wait()
-
+
+    whole_out.wait()
     pltpu.make_async_copy(
         out.at[pl.ds(0, DEV - 1), pl.ds(0, SENT)],
         out.at[pl.ds(0, DEV - 1), pl.ds(0, SENT)],
@@ -547,7 +534,7 @@
     return pl.pallas_call(
         exchange_kernel,
         out_shape=(
-            jax.ShapeDtypeStruct((DEV, SLOT, 128), F32),
+            jax.ShapeDtypeStruct((COLS // 128, ROWS, 128), F32),
             jax.ShapeDtypeStruct((ROWS, PW), F32),
             jax.ShapeDtypeStruct((COLS, PW), F32),
         ),
@@ -568,14 +555,16 @@
             pltpu.VMEM((HELD, BLK * BLK), F32),
             pltpu.VMEM((HELD, BLK, 128), F32),
             pltpu.VMEM((DEV, SLOT, 128), F32),
-            pltpu.VMEM((DEV * SLOT, 128), F32),
+            pltpu.VMEM((DEV, SLOT, 128), F32),
+            pltpu.VMEM((COLS // 128, ROWS, 128), F32),
+            pltpu.VMEM((512, 2 * DEV), BF16),
             pltpu.VMEM((ROWS, 128), F32),
             pltpu.VMEM((ROWS, 128), F32),
             pltpu.VMEM((PW, PW), F32),
             pltpu.VMEM((PW, PW), F32),
             pltpu.VMEM((128, 128), F32),
             pltpu.VMEM((128, 128), F32),
-            pltpu.VMEM((3, PW, PW), BF16),
+            pltpu.VMEM((2, PW, PW), BF16),
             pltpu.VMEM((ROWS, PW), F32),
             pltpu.SemaphoreType.DMA(()),
             pltpu.SemaphoreType.DMA(()),
@@ -587,10 +576,10 @@
             pltpu.SemaphoreType.DMA((2 * NCH,)),
             pltpu.SemaphoreType.DMA((2 * NCH,)),
             pltpu.SemaphoreType.DMA((NCH,)),
-            pltpu.SemaphoreType.DMA((8,)),
+            pltpu.SemaphoreType.DMA((9,)),
         ],
         compiler_params=pltpu.CompilerParams(
-            collective_id=0, has_side_effects=True, vmem_limit_bytes=56 << 20
+            collective_id=0, has_side_effects=True, vmem_limit_bytes=52 << 20
         ),
     )(tile_target, child_tiles, base_front)
 
@@ -600,8 +589,8 @@
 
 
 def update_kernel(
-    base_ref, recv_ref, l_ref, lc_ref, fill_ref, front_ref, factor_ref,
-    acc, tiles, lv, lcv, lc_hi, lc_lo, keep, place, todo, count, base_in, out_sem, sems
+    sum_ref, l_ref, lc_ref, fill_ref, front_ref, factor_ref,
+    acc, lv, lcv, lc_hi, lc_lo, keep, sum_in, out_sem, sems
 ):
     r = lax.axis_index("prow")
     c = lax.axis_index("pcol")
@@ -610,7 +599,13 @@
         return pl.ds(pl.multiple_of(i * STEP, STEP), STEP)
 
     def load(i):
-        return pltpu.make_async_copy(base_ref.at[0, strip(i)], acc.at[strip(i)], base_in.at[i])
+        for b in range(COLS // 128):
+            pltpu.make_async_copy(
+                sum_ref.at[b, strip(i)], acc.at[strip(i), pl.ds(b * 128, 128)], sum_in.at[i]
+            ).start()
+
+    def loaded(i):
+        return pltpu.make_async_copy(acc.at[strip(i)], acc.at[strip(i)], sum_in.at[i])
 
     def store(i):
         return pltpu.make_async_copy(acc.at[strip(i)], front_ref.at[0, strip(i)], out_sem.at[i])
@@ -620,11 +615,6 @@
     l_in = pltpu.make_async_copy(l_ref, lv, sems.at[0])
     lc_in = pltpu.make_async_copy(lc_ref, lcv, sems.at[1])
     lc_own = pltpu.make_async_copy(l_ref.at[own_rows], lcv, sems.at[1])
-    tiles_in = pltpu.make_async_copy(
-        recv_ref.at[:, pl.ds(0, BLK)], tiles.at[pl.ds(0, DEV)], sems.at[2]
-    )
-    place_in = pltpu.make_async_copy(recv_ref.at[:, BLK], place, sems.at[3])
-    place_in.start()
 
     @pl.when(r == z)
     def _():
@@ -634,11 +624,9 @@
     def _():
         lc_in.start()
 
-    load(0).start()
-    tiles_in.start()
     l_in.start()
-    for i in range(1, STEPS):
-        load(i).start()
+    for i in range(STEPS):
+        load(i)
     row_block = lax.broadcasted_iota(jnp.int32, (32, 16), 0) + 32 * r
     col_block = lax.broadcasted_iota(jnp.int32, (32, 16), 1) + 16 * c
     on = (fill_ref[0] > 0) & (row_block >= PW // BLK) & (col_block >= PW // BLK)
@@ -647,65 +635,22 @@
         == lax.broadcasted_iota(jnp.int32, (16, COLS), 0)
     ).astype(BF16)
     keep[...] = dot_nn(on.astype(BF16), spread)
-
-    for i in range(STEPS):
-        count[i] = 0
-    place_in.wait()
-
-    def sort(s, carry):
-        for u in range(2):
-            p = place[s, u * BLK].astype(jnp.int32)
-
-            @pl.when(p >= 0)
-            def _():
-                i = lax.shift_right_logical(p, 6)
-                n = count[i]
-                source = s + DEV * jnp.bitwise_and(p + u, 1)
-                todo[i * 2 * DEV + n] = source * 512 + p
-                count[i] = n + 1
-
-        return carry
-
-    lax.fori_loop(0, DEV, sort, 0)
     lc_in.wait()
     hi, lo = split2(lcv[...])
     lc_hi[...] = hi
     lc_lo[...] = lo
-    tiles_in.wait()
-
-    def swap(s, carry):
-        for u in range(4):
-            tiles[DEV + 4 * s + u] = pltpu.roll(tiles[4 * s + u], 64, 1)
-        return carry
-
-    lax.fori_loop(0, DEV // 4, swap, 0)
     l_in.wait()
-    factor_out = pltpu.make_async_copy(lv, factor_ref.at[0], sems.at[4])
+    factor_out = pltpu.make_async_copy(lv, factor_ref.at[0], sems.at[2])
     factor_out.start()
-    half = lax.broadcasted_iota(jnp.int32, (BLK, 128), 1) // BLK
 
     def rows_of(i, carry):
-        load(i).wait()
+        loaded(i).wait()
         a_hi, a_lo = split2(lv[strip(i), :])
         p = dot_nt(a_hi, lc_hi[...]) + dot_nt(a_hi, lc_lo[...]) + dot_nt(a_lo, lc_hi[...])
         for b in range(STEP // BLK):
             rows = pl.ds(pl.multiple_of(i * STEP + b * BLK, BLK), BLK)
             mask = jnp.broadcast_to(keep[pl.ds(i * (STEP // BLK) + b, 1), :], (BLK, COLS))
             acc[rows, :] = acc[rows, :] - p[b * BLK : (b + 1) * BLK, :] * mask
-
-        def add(n, carry):
-            e = todo[i * 2 * DEV + n]
-            rb = jnp.bitwise_and(lax.shift_right_logical(e, 4), 31)
-            cb = jnp.bitwise_and(lax.shift_right_logical(e, 1), 7)
-            v = jnp.where(half == jnp.bitwise_and(e, 1), tiles[lax.shift_right_logical(e, 9)], 0.0)
-            at = (
-                pl.ds(pl.multiple_of(rb * BLK, BLK), BLK),
-                pl.ds(pl.multiple_of(cb * 128, 128), 128),
-            )
-            acc[at] = acc[at] + v
-            return carry
-
-        lax.fori_loop(0, count[i], add, 0)
         store(i).start()
         return carry
 
@@ -715,38 +660,34 @@
         store(i).wait()
 
 
-def update(base_front, recv, l, lc, fill_pattern):
+def update(total, l, lc, fill_pattern):
     return pl.pallas_call(
         update_kernel,
         out_shape=(
             jax.ShapeDtypeStruct((1, ROWS, COLS), F32),
             jax.ShapeDtypeStruct((1, ROWS, PW), F32),
         ),
-        in_specs=[pl.BlockSpec(memory_space=pl.ANY)] * 4
+        in_specs=[pl.BlockSpec(memory_space=pl.ANY)] * 3
         + [pl.BlockSpec(memory_space=pltpu.VMEM)],
         out_specs=(pl.BlockSpec(memory_space=pl.ANY), pl.BlockSpec(memory_space=pl.ANY)),
         scratch_shapes=[
             pltpu.VMEM((ROWS, COLS), F32),
-            pltpu.VMEM((2 * DEV, BLK, 128), F32),
             pltpu.VMEM((ROWS, PW), F32),
             pltpu.VMEM((COLS, PW), F32),
             pltpu.VMEM((COLS, PW), BF16),
             pltpu.VMEM((COLS, PW), BF16),
             pltpu.VMEM((32, COLS), F32),
-            pltpu.SMEM((DEV, 128), F32),
-            pltpu.SMEM((STEPS * 2 * DEV,), jnp.int32),
-            pltpu.SMEM((STEPS,), jnp.int32),
             pltpu.SemaphoreType.DMA((STEPS,)),
             pltpu.SemaphoreType.DMA((STEPS,)),
-            pltpu.SemaphoreType.DMA((5,)),
+            pltpu.SemaphoreType.DMA((3,)),
         ],
-        compiler_params=pltpu.CompilerParams(vmem_limit_bytes=58 << 20),
-    )(base_front, recv, l, lc, fill_pattern)
+        compiler_params=pltpu.CompilerParams(vmem_limit_bytes=24 << 20),
+    )(total, l, lc, fill_pattern)
 
 
 def on_device(base_front, child_tiles, tile_target, fill_pattern):
-    recv, l, lc = exchange(tile_target, child_tiles, base_front)
-    front_out, factor = update(base_front, recv, l, lc, fill_pattern)
+    total, l, lc = exchange(tile_target, child_tiles, base_front)
+    front_out, factor = update(total, l, lc, fill_pattern)
     return front_out, factor
 
 

time: 125 us -> 121 us (0.968)
  Pallas kernels: 121 us -> 114 us
  local copies, waits for them, and re-layouts: 2.79 us -> 6.52 us
    pallas_call x1, Pallas kernels: 16.7 us -> 7.74 us  [update(): pl.pallas_call(update_kernel, out_shape=(jax.ShapeDtypeStruct((1, ROWS, C...]
    unnamed x2 -> x6, local copies, waits for them, and re-layouts: 2.79 us -> 6.52 us
    pallas_call x1, Pallas kernels: 104 us -> 106 us  [exchange(): pl.pallas_call(exchange_kernel, out_shape=(jax.ShapeDtypeStruct((COLS //...]
where the time goes in v2:
time: 121 us
  Pallas kernels  114 us (94%)
  local copies, waits for them, and re-layouts  6.52 us (5%)
    pallas_call x1, Pallas kernels, exchange(): pl.pallas_call(exchange_kernel, out_shape=(jax.ShapeDtypeStruct((COLS //...  106 us
    pallas_call x1, Pallas kernels, update(): pl.pallas_call(update_kernel, out_shape=(jax.ShapeDtypeStruct((1, ROWS, C...  7.74 us
    unnamed x6, local copies, waits for them, and re-layouts  6.52 us

profile of v2, /device:TPU:37, one launch (start us, length us, event | category | flops | bytes accessed | tf_op | source)
XLA Modules:
  0.0 121.1 jit_solution(740997049438143564)
XLA Ops:
  0.6 0.8 copy.7.fill_ref
  1.4 0.8 copy.6.target_ref
  2.2 106.2 %shard_map.59 = (f32[8,2048,128]{2,1,0:T(8,128)}, f32[2048,256]{1,0:T(8,128)}, f32[1024,256]{1,0:T(8,128)S(1)}) custom-call(s32[128,3]{1,0:T(8,128)S(1)} %copy.6.target_ref, f32[128,4096]{1,0:T(8,128)} %child_hbm.1, f32[1,2048,1024]{2,1,0:T(8,128)} %base_ref.1), custom_call_target="tpu_custom_call" | custom-call | tf_op jit(solution)/shard_map/pallas_call | solution.py:534
  108.4 0.0 copy-start
  108.4 3.4 %copy-done = f32[8,2048,128]{2,1,0:T(8,128)S(1)} copy-done((f32[8,2048,128]{2,1,0:T(8,128)S(1)}, f32[8,2048,128]{2,1,0:T(8,128)}, u32[]{:S(2)}) %copy-start) | copy-done | bytes 8388632
  111.8 0.0 copy-start.1
  111.8 1.6 %copy-done.1 = f32[2048,256]{1,0:T(8,128)S(1)} copy-done((f32[2048,256]{1,0:T(8,128)S(1)}, f32[2048,256]{1,0:T(8,128)}, u32[]{:S(2)}) %copy-start.1) | copy-done | bytes 2097176
  113.4 7.7 %shard_map.60 = (f32[1,2048,1024]{2,1,0:T(8,128)}, f32[1,2048,256]{2,1,0:T(8,128)}) custom-call(f32[8,2048,128]{2,1,0:T(8,128)S(1)} %copy-done, f32[2048,256]{1,0:T(8,128)S(1)} %copy-done.1, f32[1024,256]{1,0:T(8,128)S(1)} %get-tuple-element.7.lc_ref, s32[1,32,16]{2,1,0:T(8,128)S(1)} %copy.7.fill_ref), custom_call_target="tpu_custom_call" | custom-call | tf_op jit(solution)/shard_map/pallas_call | solution.py:664
Async XLA Ops:
  108.4 3.4 %copy-start = (f32[8,2048,128]{2,1,0:T(8,128)S(1)}, f32[8,2048,128]{2,1,0:T(8,128)}, u32[]{:S(2)}) copy-start(f32[8,2048,128]{2,1,0:T(8,128)} %get-tuple-element.5.sum_ref) | copy-start | bytes 25165828
  111.8 1.6 %copy-start.1 = (f32[2048,256]{1,0:T(8,128)S(1)}, f32[2048,256]{1,0:T(8,128)}, u32[]{:S(2)}) copy-start(f32[2048,256]{1,0:T(8,128)} %get-tuple-element.6.l_ref) | copy-start | bytes 6291460

commit v3 on v2

--- a/solution.py
+++ b/solution.py
@@ -13,9 +13,10 @@
 COLS = 1024
 SLOT = 72
 SENT = 65
-CHUNK = 128
-NCH = 8
-HOP = 3
+CHUNK = 64
+NCH = 16
+HOP = 4
+PRE = 2
 
 MESH = pl.DeviceIdType.MESH
 F32 = jnp.float32
@@ -53,14 +54,15 @@
 
 def slots(target_ref, meta, order, idx_v):
     t = target_ref[...]
-    target = (t[:, 0:1] * 4 + t[:, 1:2] // 32) * 8 + t[:, 2:3] // 16
-    spot = lax.rem(t[:, 1:2], 32) * 16 + lax.rem(t[:, 2:3], 16)
-    wide = jnp.broadcast_to(target, (DEV, HELD))
+    target = (t[0:1, :] * 4 + t[1:2, :] // 32) * 8 + t[2:3, :] // 16
+    spot = lax.rem(t[1:2, :], 32) * 16 + lax.rem(t[2:3, :], 16)
+    wide = jnp.broadcast_to(target, (HELD, HELD))
+    tall = wide.T
     row = lax.broadcasted_iota(jnp.int32, (HELD, HELD), 0)
     col = lax.broadcasted_iota(jnp.int32, (HELD, HELD), 1)
-    rank = jnp.sum(jnp.where((wide == wide.T) & (col < row), 1, 0), axis=1, keepdims=True)
-    here = jnp.broadcast_to(target, (HELD, DEV)) == col
-    spots = jnp.broadcast_to(spot, (HELD, DEV)) + 1
+    rank = jnp.sum(jnp.where((wide == tall) & (col < row), 1, 0), axis=1, keepdims=True)
+    here = tall == col
+    spots = jnp.broadcast_to(spot, (HELD, HELD)).T + 1
     places = []
     for u in range(2):
         hit = here & (jnp.broadcast_to(rank, (HELD, DEV)) == u)
@@ -154,18 +156,18 @@
         hot[:, u * 128 : (u + 1) * 128] = (want == there).astype(BF16)
 
 
-def add_rows(i, recv, hot, strips):
+def add_rows(i, recv, hot, strips, first=0):
     low = lax.broadcasted_iota(jnp.int32, (128, 128), 1) < BLK
     low32 = lax.broadcasted_iota(jnp.int32, (32, 128), 1) < BLK
     sides = []
     for u in range(2):
         x0 = recv[pl.ds(4 * i + 2 * u, DEV, stride=SLOT), :]
         x1 = recv[pl.ds(4 * i + 2 * u + 1, DEV, stride=SLOT), :]
-        first = jnp.where(low, x0, pltpu.roll(x1, 64, 1))
-        second = jnp.where(low, pltpu.roll(x0, 64, 1), x1)
-        sides.append(jnp.concatenate([first, second], axis=0))
+        top = jnp.where(low, x0, pltpu.roll(x1, 64, 1))
+        bottom = jnp.where(low, pltpu.roll(x0, 64, 1), x1)
+        sides.append(jnp.concatenate([top, bottom], axis=0))
     hi, lo = split2(jnp.concatenate(sides, axis=1))
-    mark = hot[0 : 64 * len(strips), :]
+    mark = hot[64 * first : 64 * (first + len(strips)), :]
     y = dot_nn(mark, hi) + dot_nn(mark, lo)
     for u in range(2):
         part = y[:, u * 128 : (u + 1) * 128]
@@ -401,25 +403,26 @@
 
         mark_places(recv, hot)
 
-        def panel_rows(i, carry):
-            add_rows(i, recv, hot, (panel0, panel1))
-            return carry
-
-        lax.fori_loop(0, BLK // 4, panel_rows, 0)
-
-        def produce(k, carry):
-            top, bottom = piece(0, k), piece(1, k)
+        def produce(k):
+            add_rows(k, recv, hot, (panel0, panel1))
             p = jnp.concatenate(
                 [
-                    jnp.concatenate([panel0[top, :], panel0[bottom, :]], axis=0),
-                    jnp.concatenate([panel1[top, :], panel1[bottom, :]], axis=0),
+                    jnp.concatenate(
+                        [
+                            panel[pl.ds(half * COLS + 4 * k + u, 16, stride=BLK), :]
+                            for half in range(2)
+                            for u in range(4)
+                        ],
+                        axis=0,
+                    )
+                    for panel in (panel0, panel1)
                 ],
                 axis=1,
             )
             p_hi, p_lo = split2(p)
             y = dot_nn(p_hi, ms[0]) + dot_nn(p_hi, ms[1]) + dot_nn(p_lo, ms[0])
-            lv[top, :] = y[:CHUNK]
-            lv[bottom, :] = y[CHUNK:]
+            lv[piece(0, k), :] = y[:CHUNK]
+            lv[piece(1, k), :] = y[CHUNK:]
             for half in range(2):
                 z_next(lv, half, k).start()
                 cross(lv, half, k, (oth_recv, own_recv)[half].at[k]).start()
@@ -428,22 +431,33 @@
             def _():
                 x_hop(lv.at[piece(0, k)], k).start()
 
+        last = NCH + 3 * HOP
+        start = last - BLK // 4
+        whole_in.wait()
+
+        def factor_step(t, carry):
+            @pl.when(t < NCH)
+            def _():
+                produce(t)
+
+            x_due(t)
+
+            @pl.when(t >= start)
+            def _():
+                add_rows(t - start, recv, hot, strips[2:], first=2)
+
             return carry
 
-        lax.fori_loop(0, NCH, produce, 0)
+        lax.fori_loop(0, last, factor_step, 0)
         keep.start()
-        whole_in.wait()
-
-        def own_rows(t, carry):
-            x_due(t)
-
-            @pl.when(t < BLK // 4)
-            def _():
-                add_rows(t, recv, hot, strips)
-
+
+        def panel_back(i, carry):
+            rows = pl.ds(pl.multiple_of(i * 256, 256), 256)
+            acc[0, rows, :] = panel0[rows, :]
+            acc[1, rows, :] = panel1[rows, :]
             return carry
 
-        lax.fori_loop(0, max(BLK // 4, NCH + 3 * HOP), own_rows, 0)
+        lax.fori_loop(0, ROWS // 256, panel_back, 0)
         whole_out.start()
 
     z_forwards = ((h == 0) & ((z == 1) | (z == 2))) | ((h == 1) & ((z == 3) | (z == 2)))
@@ -454,12 +468,11 @@
         whole_in.wait()
         mark_places(recv, hot)
 
-        def own_rows(i, carry):
+        def early_rows(i, carry):
             add_rows(i, recv, hot, strips)
             return carry
 
-        lax.fori_loop(0, BLK // 4, own_rows, 0)
-        whole_out.start()
+        lax.fori_loop(0, PRE, early_rows, 0)
 
         def relay(t, carry):
             @pl.when(t < NCH)
@@ -480,6 +493,15 @@
                     cross(l_ref, h, k, oth_recv.at[k]).start()
 
             x_due(t)
+
+            @pl.when(t < BLK // 4 - PRE)
+            def _():
+                add_rows(t + PRE, recv, hot, strips)
+
+            @pl.when(t == BLK // 4 - PRE)
+            def _():
+                whole_out.start()
+
             return carry
 
         lax.fori_loop(0, NCH + 3 * HOP, relay, 0)
@@ -579,7 +601,7 @@
             pltpu.SemaphoreType.DMA((9,)),
         ],
         compiler_params=pltpu.CompilerParams(
-            collective_id=0, has_side_effects=True, vmem_limit_bytes=52 << 20
+            collective_id=0, has_side_effects=True, vmem_limit_bytes=40 << 20
         ),
     )(tile_target, child_tiles, base_front)
 
@@ -590,7 +612,7 @@
 
 def update_kernel(
     sum_ref, l_ref, lc_ref, fill_ref, front_ref, factor_ref,
-    acc, lv, lcv, lc_hi, lc_lo, keep, sum_in, out_sem, sems
+    acc, lv, lcv, ln, lcn, lc_hi, lc_lo, keep, sum_in, out_sem, sems
 ):
     r = lax.axis_index("prow")
     c = lax.axis_index("pcol")
@@ -627,25 +649,45 @@
     l_in.start()
     for i in range(STEPS):
         load(i)
-    row_block = lax.broadcasted_iota(jnp.int32, (32, 16), 0) + 32 * r
-    col_block = lax.broadcasted_iota(jnp.int32, (32, 16), 1) + 16 * c
+    row_block = lax.broadcasted_iota(jnp.int32, (16, 32), 1) + 32 * r
+    col_block = lax.broadcasted_iota(jnp.int32, (16, 32), 0) + 16 * c
     on = (fill_ref[0] > 0) & (row_block >= PW // BLK) & (col_block >= PW // BLK)
     spread = (
         lax.broadcasted_iota(jnp.int32, (16, COLS), 1) // BLK
         == lax.broadcasted_iota(jnp.int32, (16, COLS), 0)
     ).astype(BF16)
-    keep[...] = dot_nn(on.astype(BF16), spread)
+    keep[...] = lax.dot_general(
+        on.astype(BF16), spread, (((0,), (0,)), ((), ())), preferred_element_type=F32
+    )
     lc_in.wait()
-    hi, lo = split2(lcv[...])
+
+    def settle(raw, halves, natural):
+        def rows_back(i, carry):
+            for half in range(halves):
+                for j in range(2):
+                    natural.at[j][pl.ds(half * COLS + i, 16, stride=BLK), :] = raw[
+                        pl.ds(pl.multiple_of(half * COLS + 16 * i, 16), 16), j * 128 : (j + 1) * 128
+                    ]
+            return carry
+
+        lax.fori_loop(0, BLK, rows_back, 0, unroll=4)
+
+    settle(lcv, 1, lcn)
+    hi, lo = split2(jnp.concatenate([lcn[0], lcn[1]], axis=1))
     lc_hi[...] = hi
     lc_lo[...] = lo
     l_in.wait()
-    factor_out = pltpu.make_async_copy(lv, factor_ref.at[0], sems.at[2])
-    factor_out.start()
+    settle(lv, 2, ln)
+    factor_out = [
+        pltpu.make_async_copy(ln.at[j], factor_ref.at[0, :, pl.ds(j * 128, 128)], sems.at[2 + j])
+        for j in range(2)
+    ]
+    for j in range(2):
+        factor_out[j].start()
 
     def rows_of(i, carry):
         loaded(i).wait()
-        a_hi, a_lo = split2(lv[strip(i), :])
+        a_hi, a_lo = split2(jnp.concatenate([ln[0, strip(i), :], ln[1, strip(i), :]], axis=1))
         p = dot_nt(a_hi, lc_hi[...]) + dot_nt(a_hi, lc_lo[...]) + dot_nt(a_lo, lc_hi[...])
         for b in range(STEP // BLK):
             rows = pl.ds(pl.multiple_of(i * STEP + b * BLK, BLK), BLK)
@@ -655,7 +697,8 @@
         return carry
 
     lax.fori_loop(0, STEPS, rows_of, 0)
-    factor_out.wait()
+    for j in range(2):
+        factor_out[j].wait()
     for i in range(STEPS):
         store(i).wait()
 
@@ -674,20 +717,22 @@
             pltpu.VMEM((ROWS, COLS), F32),
             pltpu.VMEM((ROWS, PW), F32),
             pltpu.VMEM((COLS, PW), F32),
+            pltpu.VMEM((2, ROWS, 128), F32),
+            pltpu.VMEM((2, COLS, 128), F32),
             pltpu.VMEM((COLS, PW), BF16),
             pltpu.VMEM((COLS, PW), BF16),
             pltpu.VMEM((32, COLS), F32),
             pltpu.SemaphoreType.DMA((STEPS,)),
             pltpu.SemaphoreType.DMA((STEPS,)),
-            pltpu.SemaphoreType.DMA((3,)),
+            pltpu.SemaphoreType.DMA((4,)),
         ],
         compiler_params=pltpu.CompilerParams(vmem_limit_bytes=24 << 20),
     )(total, l, lc, fill_pattern)
 
 
 def on_device(base_front, child_tiles, tile_target, fill_pattern):
-    total, l, lc = exchange(tile_target, child_tiles, base_front)
-    front_out, factor = update(total, l, lc, fill_pattern)
+    total, l, lc = exchange(tile_target.T, child_tiles, base_front)
+    front_out, factor = update(total, l, lc, fill_pattern.transpose(0, 2, 1))
     return front_out, factor
 
 

time: 121 us -> 112 us (0.926); the launches traced: 121 us -> 110 us
  Pallas kernels: 114 us -> 107 us
  local copies, waits for them, and re-layouts: 6.52 us -> 2.27 us
    pallas_call x1, Pallas kernels: 106 us -> 95.9 us  [exchange(): pl.pallas_call(exchange_kernel, out_shape=(jax.ShapeDtypeStruct((COLS //...]
    unnamed x6, local copies, waits for them, and re-layouts: 6.52 us -> 2.27 us
    pallas_call x1, Pallas kernels: 7.74 us -> 11 us  [update(): pl.pallas_call(update_kernel, out_shape=(jax.ShapeDtypeStruct((1, ROWS, C...]
where the time goes in v3:
time: 112 us; the launch traced here: 110 us
  Pallas kernels  107 us (96%)
  local copies, waits for them, and re-layouts  2.27 us (2%)
    pallas_call x1, Pallas kernels, exchange(): pl.pallas_call(exchange_kernel, out_shape=(jax.ShapeDtypeStruct((COLS //...  95.9 us
    pallas_call x1, Pallas kernels, update(): pl.pallas_call(update_kernel, out_shape=(jax.ShapeDtypeStruct((1, ROWS, C...  11 us
    unnamed x6, local copies, waits for them, and re-layouts  2.27 us

profile of v3, /device:TPU:37, one launch (start us, length us, event | category | flops | bytes accessed | tf_op | source)
XLA Modules:
  0.0 109.8 jit_solution(8325291156741842173)
XLA Ops:
  0.6 0.0 copy-start
  0.6 1.6 %copy-done = f32[128,4096]{1,0:T(8,128)S(1)} copy-done((f32[128,4096]{1,0:T(8,128)S(1)}, f32[128,4096]{1,0:T(8,128)}, u32[]{:S(2)}) %copy-start) | copy-done | bytes 2097176
  2.2 0.0 copy-start.2
  2.2 0.7 copy-done.2
  2.9 0.0 copy-start.1
  2.9 95.9 %shard_map.59 = (f32[8,2048,128]{2,1,0:T(8,128)S(1)}, f32[2048,256]{1,0:T(8,128)S(1)}, f32[1024,256]{1,0:T(8,128)S(1)}) custom-call(s32[3,128]{1,0:T(4,128)S(1)} %bitcast.3, f32[128,4096]{1,0:T(8,128)S(1)} %copy-done, f32[1,2048,1024]{2,1,0:T(8,128)} %base_ref.1), custom_call_target="tpu_custom_call" | custom-call | tf_op jit(solution)/shard_map/pallas_call | solution.py:556
  98.8 0.0 copy-done.1
  98.8 11.0 %shard_map.60 = (f32[1,2048,1024]{2,1,0:T(8,128)}, f32[1,2048,256]{2,1,0:T(8,128)}) custom-call(f32[8,2048,128]{2,1,0:T(8,128)S(1)} %get-tuple-element.5.sum_ref, f32[2048,256]{1,0:T(8,128)S(1)} %get-tuple-element.6.l_ref, f32[1024,256]{1,0:T(8,128)S(1)} %get-tuple-element.7.lc_ref, s32[1,16,32]{2,1,0:T(8,128)S(1)} %bitcast.2), custom_call_target="tpu_custom_call" | custom-call | tf_op jit(solution)/shard_map/pallas_call | solution.py:707
Async XLA Ops:
  0.6 1.6 %copy-start = (f32[128,4096]{1,0:T(8,128)S(1)}, f32[128,4096]{1,0:T(8,128)}, u32[]{:S(2)}) copy-start(f32[128,4096]{1,0:T(8,128)} %child_hbm.1) | copy-start | bytes 6291460
  2.2 0.7 copy-start.2
  2.9 95.9 %copy-start.1 = (s32[1,32,16]{1,2,0:T(8,128)S(1)}, s32[1,32,16]{1,2,0:T(8,128)}, u32[]{:S(2)}) copy-start(s32[1,32,16]{1,2,0:T(8,128)} %param.7) | copy-start | bytes 6148

commit v4 on v3

--- a/solution.py
+++ b/solution.py
@@ -670,7 +670,7 @@
                     ]
             return carry
 
-        lax.fori_loop(0, BLK, rows_back, 0, unroll=4)
+        lax.fori_loop(0, BLK, rows_back, 0, unroll=16)
 
     settle(lcv, 1, lcn)
     hi, lo = split2(jnp.concatenate([lcn[0], lcn[1]], axis=1))

time: 112 us -> 112 us (level)
  no operation moved by 1% of the time
where the time goes in v4:
time: 112 us; the launch traced here: 110 us
  Pallas kernels  107 us (96%)
  local copies, waits for them, and re-layouts  2.27 us (2%)
    pallas_call x1, Pallas kernels, exchange(): pl.pallas_call(exchange_kernel, out_shape=(jax.ShapeDtypeStruct((COLS //...  95.9 us
    pallas_call x1, Pallas kernels, update(): pl.pallas_call(update_kernel, out_shape=(jax.ShapeDtypeStruct((1, ROWS, C...  11 us
    unnamed x6, local copies, waits for them, and re-layouts  2.27 us

profile of v4, /device:TPU:37, one launch (start us, length us, event | category | flops | bytes accessed | tf_op | source)
XLA Modules:
  0.0 109.8 jit_solution(1771517260644470546)
XLA Ops:
  0.6 0.0 copy-start
  0.6 1.6 %copy-done = f32[128,4096]{1,0:T(8,128)S(1)} copy-done((f32[128,4096]{1,0:T(8,128)S(1)}, f32[128,4096]{1,0:T(8,128)}, u32[]{:S(2)}) %copy-start) | copy-done | bytes 2097176
  2.2 0.0 copy-start.2
  2.2 0.7 copy-done.2
  2.9 0.0 copy-start.1
  2.9 95.9 %shard_map.59 = (f32[8,2048,128]{2,1,0:T(8,128)S(1)}, f32[2048,256]{1,0:T(8,128)S(1)}, f32[1024,256]{1,0:T(8,128)S(1)}) custom-call(s32[3,128]{1,0:T(4,128)S(1)} %bitcast.3, f32[128,4096]{1,0:T(8,128)S(1)} %copy-done, f32[1,2048,1024]{2,1,0:T(8,128)} %base_ref.1), custom_call_target="tpu_custom_call" | custom-call | tf_op jit(solution)/shard_map/pallas_call | solution.py:556
  98.8 0.0 copy-done.1
  98.8 11.0 %shard_map.60 = (f32[1,2048,1024]{2,1,0:T(8,128)}, f32[1,2048,256]{2,1,0:T(8,128)}) custom-call(f32[8,2048,128]{2,1,0:T(8,128)S(1)} %get-tuple-element.5.sum_ref, f32[2048,256]{1,0:T(8,128)S(1)} %get-tuple-element.6.l_ref, f32[1024,256]{1,0:T(8,128)S(1)} %get-tuple-element.7.lc_ref, s32[1,16,32]{2,1,0:T(8,128)S(1)} %bitcast.2), custom_call_target="tpu_custom_call" | custom-call | tf_op jit(solution)/shard_map/pallas_call | solution.py:707
Async XLA Ops:
  0.6 1.6 %copy-start = (f32[128,4096]{1,0:T(8,128)S(1)}, f32[128,4096]{1,0:T(8,128)}, u32[]{:S(2)}) copy-start(f32[128,4096]{1,0:T(8,128)} %child_hbm.1) | copy-start | bytes 6291460
  2.2 0.7 copy-start.2
  2.9 95.9 %copy-start.1 = (s32[1,32,16]{1,2,0:T(8,128)S(1)}, s32[1,32,16]{1,2,0:T(8,128)}, u32[]{:S(2)}) copy-start(s32[1,32,16]{1,2,0:T(8,128)} %param.7) | copy-start | bytes 6148
